TPU v7x, 256 devices: a whole 4x4x8 slice. The times are simulated.
256 devices in a mesh: fsdp: 32 (over y, x, core), tp: 8 (over z).
Axes of the slice: x: 4, y: 4, z: 8, core: 2. Of those that a mesh axis runs over, the one named last changes fastest.
Arguments:
- learner_flat: bfloat16 [2, 159383552], P(None, ('fsdp', 'tp')), may hold values from -1.796875 to 1.796875
- param_offsets: int32 [2, 128, 4], replicated, may hold values from 0 to 622336, as said below
- owner_map: int32 [2, 128], replicated, may hold values from 0 to 31, as said below
- slice_map: int32 [32, 8], replicated, may hold values from 0 to 7, each once within a row
Outputs:
- query_absorbed: bfloat16 [2, 128, 1536, 512], P(None, 'fsdp', 'tp')
- output_absorbed: bfloat16 [2, 128, 7168, 512], P(None, 'fsdp', 'tp')
Inputs may be any that keep to these rules, and one draw needn't show every extreme that they name: `param_offsets`: in each layer the pieces of all heads' four parameters lie in a rank's 622592 entries one after another in some order, without gaps or intersections; a piece of a parameter holds that parameter's entries divided by 256; the last piece of each layer is a key up-projection piece. `owner_map`: in each layer every index of fsdp owns exactly 4 heads.
All inputs are finite; a program needn't handle non-finite values.
Results may differ from a plain program's by a relative error of at most 0.001.
Values may be sent and summed in bfloat16 or wider, within the bound.
A program may use at most 64 MiB of HBM per device.

v0:
```python
import math

import jax
import jax.numpy as jnp
from jax import lax
from jax.sharding import PartitionSpec as P

D = 7168
QR = 1536
KVR = 512
QK_NOPE = 128
V_DIM = 128


def for_sending(shard):
    return jax.tree.map(lambda a: a.astype(jnp.bfloat16) if a.dtype == jnp.float32 else a, shard)


def head_order(owner_map, per_group):
    head_count = owner_map.shape[1]
    head_index = jnp.arange(head_count, dtype=jnp.int32)
    same_owner = owner_map[:, :, None] == owner_map[:, None, :]
    before = head_index[None, None, :] < head_index[None, :, None]
    head_rank = jnp.sum(jnp.logical_and(same_owner, before).astype(jnp.int32), axis=2)
    head_slot = owner_map * per_group + head_rank
    slot_hits = head_slot[:, :, None] == head_index[None, None, :]
    return jnp.sum(jnp.where(slot_hits, head_index[None, :, None], 0), axis=1)


def cut_pieces(local_flat, begins, width_now, granule):
    layer_count, heads_here = begins.shape
    row_table = local_flat.reshape(layer_count, local_flat.shape[1] // granule, granule)
    row_steps = jnp.arange(width_now // granule, dtype=jnp.int32)
    row_ids = (begins[:, :, None] // granule + row_steps[None, None, :]).reshape(
        layer_count, heads_here * (width_now // granule)
    )
    picked = jnp.take_along_axis(row_table, row_ids[:, :, None], axis=1)
    return picked.reshape(layer_count, heads_here, width_now)


def refresh(local_flat, param_offsets, head_at, slice_row):
    fsdp_ways = lax.axis_size("fsdp")
    tensor_ways = lax.axis_size("tp")
    rank_total = fsdp_ways * tensor_ways
    layer_count = local_flat.shape[0]
    per_group = head_at.shape[1] // fsdp_ways
    widths = (
        QR * QK_NOPE // rank_total,
        QK_NOPE * KVR // rank_total,
        V_DIM * KVR // rank_total,
        D * V_DIM // rank_total,
    )
    granule = math.gcd(math.gcd(widths[0], widths[1]), math.gcd(widths[2], widths[3]))
    begins = jnp.take_along_axis(param_offsets, head_at[:, :, None], axis=1)
    pieces = tuple(
        (
            cut_pieces(local_flat, begins[:, :, kind_id], widths[kind_id], granule).reshape(
                layer_count, fsdp_ways, per_group, 1, widths[kind_id]
            )
            for kind_id in range(4)
        )
    )
    arrived = jax.tree.map(
        lambda part, own: part.astype(own.dtype),
        lax.all_to_all(for_sending(pieces), "fsdp", split_axis=1, concat_axis=3, tiled=True),
        pieces,
    )
    query_part, key_part, value_part, out_part = tuple(
        (
            arrived[kind_id].reshape(layer_count, per_group, fsdp_ways, 1, widths[kind_id])
            for kind_id in range(4)
        )
    )
    slice_query = QR // tensor_ways
    slice_output = D // tensor_ways
    blocks = fsdp_ways // tensor_ways

    def to_send(part_in, width_now):
        grouped = part_in.reshape(layer_count, per_group, tensor_ways, blocks, width_now)
        return jnp.take(grouped, slice_row, axis=2).reshape(
            layer_count, per_group, tensor_ways, blocks, 1, width_now
        )

    query_rows, out_rows = (
        lax.all_to_all(
            to_send(query_part, widths[0]), "tp", split_axis=2, concat_axis=4, tiled=True
        ),
        lax.all_to_all(to_send(out_part, widths[3]), "tp", split_axis=2, concat_axis=4, tiled=True),
    )
    query_rows = query_rows.reshape(layer_count, per_group, slice_query, QK_NOPE)
    out_rows = out_rows.reshape(layer_count, per_group, slice_output, V_DIM)
    key_full, value_full = (
        lax.all_gather(key_part, "tp", axis=3, tiled=True),
        lax.all_gather(value_part, "tp", axis=3, tiled=True),
    )
    key_full = key_full.reshape(layer_count, per_group, QK_NOPE, KVR)
    value_full = value_full.reshape(layer_count, per_group, V_DIM, KVR)
    query_absorbed = jnp.einsum(
        "lhrc,lhck->lhrk", query_rows, key_full, preferred_element_type=jnp.float32
    ).astype(jnp.bfloat16)
    output_absorbed = jnp.einsum(
        "lhrc,lhck->lhrk", out_rows, value_full, preferred_element_type=jnp.float32
    ).astype(jnp.bfloat16)
    return (query_absorbed, output_absorbed)


def per_device(learner_flat, param_offsets, owner_map, slice_map):
    fsdp_ways = lax.axis_size("fsdp")
    per_group = owner_map.shape[1] // fsdp_ways
    head_at = head_order(owner_map, per_group)
    slice_row = lax.dynamic_index_in_dim(slice_map, lax.axis_index("fsdp"), 0, keepdims=False)
    layer_results = [
        refresh(
            learner_flat[layer_id : layer_id + 1],
            param_offsets[layer_id : layer_id + 1],
            head_at[layer_id : layer_id + 1],
            slice_row,
        )
        for layer_id in range(learner_flat.shape[0])
    ]
    query_absorbed = jnp.concatenate([result_pair[0] for result_pair in layer_results], axis=0)
    output_absorbed = jnp.concatenate([result_pair[1] for result_pair in layer_results], axis=0)
    return (query_absorbed, output_absorbed)


def solution(mesh):
    placed = (P(None, ("fsdp", "tp")), P(), P(), P())
    return jax.shard_map(
        per_device,
        mesh=mesh,
        in_specs=placed,
        out_specs=(P(None, "fsdp", "tp", None), P(None, "fsdp", "tp", None)),
        check_vma=False,
    )
```

profile of v0, /device:TPU:38, one launch (start us, length us, event | category | flops | bytes accessed | tf_op | source)
XLA Modules:
  0.0 371.7 jit_solution(2697430013469942218)
XLA Ops:
  4.4 28.8 %slice_reduce_fusion.1 = (bf16[622592]{0:T(1024)(128)(2,1)S(1)}, bf16[622592]{0:T(1024)(128)(2,1)}) fusion(bf16[2,622592]{1,0:T(2,128)(2,1)} %param.16), kind=kLoop, calls=%fused_computation.18 | loop fusion | bytes 4980736 | tf_op jit(solution)/shard_map/slice | solution.py:114
  35.2 7.6 %all-to-all-start.8 = ((bf16[1,32,4,1,256]{4,2,3,0,1:T(4,128)(2,1)}), bf16[1,32,4,1,256]{4,2,3,0,1:T(4,128)(2,1)S(1)}, u32[]{:S(2)}, u32[]{:S(2)}) async-start(bf16[1,32,4,1,256]{4,2,3,0,1:T(4,128)(2,1)} %bitcast.57), calls=%async_computation.8 | async-start | bytes 131072 | tf_op jit(solution)/shard_map/all_to_all | solution.py:65
  55.8 7.4 %all-to-all-start.2 = ((bf16[1,32,4,1,256]{4,2,3,0,1:T(4,128)(2,1)}), bf16[1,32,4,1,256]{4,2,3,0,1:T(4,128)(2,1)S(1)}, u32[]{:S(2)}, u32[]{:S(2)}) async-start(bf16[1,32,4,1,256]{4,2,3,0,1:T(4,128)(2,1)} %bitcast.18), calls=%async_computation.2 | async-start | bytes 131072 | tf_op jit(solution)/shard_map/all_to_all | solution.py:65
  68.9 6.2 %all-to-all-start.11 = ((bf16[1,32,4,1,256]{4,2,3,0,1:T(4,128)(2,1)}), bf16[1,32,4,1,256]{4,2,3,0,1:T(4,128)(2,1)}, u32[]{:S(2)}, u32[]{:S(2)}) async-start(bf16[1,32,4,1,256]{4,2,3,0,1:T(4,128)(2,1)} %bitcast.74), calls=%async_computation.11 | async-start | bytes 131072 | tf_op jit(solution)/shard_map/all_to_all | solution.py:65
  75.1 5.5 %gather_fusion.8 = bf16[1792,256]{1,0:T(8,128)(2,1)S(1)} fusion(bf16[2432,256]{1,0:T(8,128)(2,1)S(1)} %reshape.643, s32[2048]{0:T(1024)S(1)} %pad_clamp_fusion.1), kind=kCustom, calls=%fused_computation.4.clone | custom fusion | bytes 1842176 | tf_op jit(solution)/shard_map/jit(take_along_axis)/gather | solution.py:37
  83.8 7.5 %all-to-all-start.5 = ((bf16[1,32,4,1,256]{4,2,3,0,1:T(4,128)(2,1)}), bf16[1,32,4,1,256]{4,2,3,0,1:T(4,128)(2,1)S(1)}, u32[]{:S(2)}, u32[]{:S(2)}) async-start(bf16[1,32,4,1,256]{4,2,3,0,1:T(4,128)(2,1)} %bitcast.40), calls=%async_computation.5 | async-start | bytes 131072 | tf_op jit(solution)/shard_map/all_to_all | solution.py:65
  97.6 5.6 %all-to-all-start = ((bf16[1,32,4,1,768]{4,2,3,0,1:T(4,128)(2,1)}), bf16[1,32,4,1,768]{4,2,3,0,1:T(4,128)(2,1)S(1)}, u32[]{:S(2)}, u32[]{:S(2)}) async-start(bf16[1,32,4,1,768]{4,2,3,0,1:T(4,128)(2,1)} %bitcast.6), calls=%async_computation | async-start | bytes 393216 | tf_op jit(solution)/shard_map/all_to_all | solution.py:65
  104.1 5.7 %all-to-all-done = bf16[1,32,4,1,768]{4,2,3,0,1:T(4,128)(2,1)S(1)} async-done(((bf16[1,32,4,1,768]{4,2,3,0,1:T(4,128)(2,1)}), bf16[1,32,4,1,768]{4,2,3,0,1:T(4,128)(2,1)S(1)}, u32[]{:S(2)}, u32[]{:S(2)}) %all-to-all-start) | async-done | bytes 196640 | tf_op jit(solution)/shard_map/all_to_all | solution.py:65
  109.8 5.5 %all-to-all-start.3 = ((bf16[1,32,4,1,768]{4,2,3,0,1:T(4,128)(2,1)}), bf16[1,32,4,1,768]{4,2,3,0,1:T(4,128)(2,1)S(1)}, u32[]{:S(2)}, u32[]{:S(2)}) async-start(bf16[1,32,4,1,768]{4,2,3,0,1:T(4,128)(2,1)} %bitcast.28), calls=%async_computation.3 | async-start | bytes 393216 | tf_op jit(solution)/shard_map/all_to_all | solution.py:65
  116.9 4.9 %all-to-all-done.3 = bf16[1,32,4,1,768]{4,2,3,0,1:T(4,128)(2,1)S(1)} async-done(((bf16[1,32,4,1,768]{4,2,3,0,1:T(4,128)(2,1)}), bf16[1,32,4,1,768]{4,2,3,0,1:T(4,128)(2,1)S(1)}, u32[]{:S(2)}, u32[]{:S(2)}) %all-to-all-start.3) | async-done | bytes 196640 | tf_op jit(solution)/shard_map/all_to_all | solution.py:65
  121.9 5.5 %all-to-all-start.6 = ((bf16[1,32,4,1,3584]{4,2,3,0,1:T(4,128)(2,1)}), bf16[1,32,4,1,3584]{4,2,3,0,1:T(4,128)(2,1)S(1)}, u32[]{:S(2)}, u32[]{:S(2)}) async-start(bf16[1,32,4,1,3584]{4,2,3,0,1:T(4,128)(2,1)} %bitcast.45), calls=%async_computation.6 | async-start | bytes 1835008 | tf_op jit(solution)/shard_map/all_to_all | solution.py:65
  127.4 5.5 %gather_fusion.11 = bf16[1792,256]{1,0:T(8,128)(2,1)S(1)} fusion(bf16[2432,256]{1,0:T(8,128)(2,1)S(1)} %reshape.662, s32[2048]{0:T(1024)S(1)} %pad_clamp_fusion), kind=kCustom, calls=%fused_computation.12.clone | custom fusion | bytes 1842176 | tf_op jit(solution)/shard_map/jit(take_along_axis)/gather | solution.py:37
  134.5 6.2 %all-to-all-done.6 = bf16[1,32,4,1,3584]{4,2,3,0,1:T(4,128)(2,1)S(1)} async-done(((bf16[1,32,4,1,3584]{4,2,3,0,1:T(4,128)(2,1)}), bf16[1,32,4,1,3584]{4,2,3,0,1:T(4,128)(2,1)S(1)}, u32[]{:S(2)}, u32[]{:S(2)}) %all-to-all-start.6) | async-done | bytes 917536 | tf_op jit(solution)/shard_map/all_to_all | solution.py:65
  140.7 6.4 %all-to-all-start.9 = ((bf16[1,32,4,1,3584]{4,2,3,0,1:T(4,128)(2,1)}), bf16[1,32,4,1,3584]{4,2,3,0,1:T(4,128)(2,1)S(1)}, u32[]{:S(2)}, u32[]{:S(2)}) async-start(bf16[1,32,4,1,3584]{4,2,3,0,1:T(4,128)(2,1)} %bitcast.62), calls=%async_computation.9 | async-start | bytes 1835008 | tf_op jit(solution)/shard_map/all_to_all | solution.py:65
  149.9 10.5 %all-to-all-done.9 = bf16[1,32,4,1,3584]{4,2,3,0,1:T(4,128)(2,1)S(1)} async-done(((bf16[1,32,4,1,3584]{4,2,3,0,1:T(4,128)(2,1)}), bf16[1,32,4,1,3584]{4,2,3,0,1:T(4,128)(2,1)S(1)}, u32[]{:S(2)}, u32[]{:S(2)}) %all-to-all-start.9) | async-done | bytes 917536 | tf_op jit(solution)/shard_map/all_to_all | solution.py:65
  160.5 8.6 %all-to-all-start.1 = ((bf16[1,4,8,4,1,768]{5,3,1,4,0,2:T(4,128)(2,1)}), bf16[1,4,8,4,1,768]{5,3,1,4,0,2:T(4,128)(2,1)S(1)}, u32[]{:S(2)}, u32[]{:S(2)}) async-start(bf16[1,4,8,4,1,768]{5,3,1,4,0,2:T(4,128)(2,1)} %get-tuple-element.46), calls=%async_computation.1 | async-start | bytes 393216 | tf_op jit(solution)/shard_map/all_to_all | solution.py:85
  172.4 7.0 %all-to-all-done.1 = bf16[1,4,8,4,1,768]{5,3,1,4,0,2:T(4,128)(2,1)S(1)} async-done(((bf16[1,4,8,4,1,768]{5,3,1,4,0,2:T(4,128)(2,1)}), bf16[1,4,8,4,1,768]{5,3,1,4,0,2:T(4,128)(2,1)S(1)}, u32[]{:S(2)}, u32[]{:S(2)}) %all-to-all-start.1) | async-done | bytes 196640 | tf_op jit(solution)/shard_map/all_to_all | solution.py:85
  186.0 7.8 %all-to-all-done.4 = bf16[1,4,8,4,1,768]{5,3,1,4,0,2:T(4,128)(2,1)S(1)} async-done(((bf16[1,4,8,4,1,768]{5,3,1,4,0,2:T(4,128)(2,1)}), bf16[1,4,8,4,1,768]{5,3,1,4,0,2:T(4,128)(2,1)S(1)}, u32[]{:S(2)}, u32[]{:S(2)}) %all-to-all-start.4) | async-done | bytes 196640 | tf_op jit(solution)/shard_map/all_to_all | solution.py:85
  193.8 27.8 %all_to_all.180 = bf16[1,4,8,4,1,3584]{5,3,1,4,0,2:T(4,128)(2,1)S(1)} all-to-all(bf16[1,4,8,4,1,3584]{5,3,1,4,0,2:T(4,128)(2,1)S(1)} %get-tuple-element.44), channel_id=1, replica_groups=mesh['fsdp'=32,'tp'=8] {'tp'}, dimensions={2} | all-to-all | bytes 1835008 | tf_op jit(solution)/shard_map/all_to_all | solution.py:88
  221.6 4.9 %all-to-all-start.10 = ((bf16[1,4,8,4,1,3584]{5,3,1,4,0,2:T(4,128)(2,1)}), bf16[1,4,8,4,1,3584]{5,3,1,4,0,2:T(4,128)(2,1)S(1)}, u32[]{:S(2)}, u32[]{:S(2)}) async-start(bf16[1,4,8,4,1,3584]{5,3,1,4,0,2:T(4,128)(2,1)} %get-tuple-element.45), calls=%async_computation.10 | async-start | bytes 1835008 | tf_op jit(solution)/shard_map/all_to_all | solution.py:88
  226.5 41.6 %all-gather = bf16[1,1,4,32,8,256]{5,3,4,2,1,0:T(8,128)(2,1)S(1)} all-gather(bf16[1,1,4,32,1,256]{5,3,4,2,1,0:T(8,128)(2,1)S(1)} %bitcast.216), channel_id=2, replica_groups=mesh['fsdp'=32,'tp'=8] {'tp'}, dimensions={4}, use_global_device_ids=true | all-gather | bytes 589824 | tf_op jit(solution)/shard_map/all_gather | solution.py:93
  268.6 25.5 %all-gather.2 = bf16[1,1,4,32,8,256]{5,3,4,2,1,0:T(8,128)(2,1)S(1)} all-gather(bf16[1,1,4,32,1,256]{5,3,4,2,1,0:T(8,128)(2,1)S(1)} %bitcast.217), channel_id=4, replica_groups=mesh['fsdp'=32,'tp'=8] {'tp'}, dimensions={4}, use_global_device_ids=true | all-gather | bytes 589824 | tf_op jit(solution)/shard_map/all_gather | solution.py:94
  294.6 25.5 %all-gather.1 = bf16[1,1,4,32,8,256]{5,3,4,2,1,0:T(8,128)(2,1)S(1)} all-gather(bf16[1,1,4,32,1,256]{5,3,4,2,1,0:T(8,128)(2,1)S(1)} %bitcast.218), channel_id=3, replica_groups=mesh['fsdp'=32,'tp'=8] {'tp'}, dimensions={4}, use_global_device_ids=true | all-gather | bytes 589824 | tf_op jit(solution)/shard_map/all_gather | solution.py:93
  323.3 25.2 %all-gather.3 = bf16[1,1,4,32,8,256]{5,3,4,2,1,0:T(8,128)(2,1)S(1)} all-gather(bf16[1,1,4,32,1,256]{5,3,4,2,1,0:T(8,128)(2,1)S(1)} %bitcast.219), channel_id=5, replica_groups=mesh['fsdp'=32,'tp'=8] {'tp'}, dimensions={4}, use_global_device_ids=true | all-gather | bytes 589824 | tf_op jit(solution)/shard_map/all_gather | solution.py:94
  (146 shorter events, 78.1 us)
Async XLA Ops:
  0.6 146.5 %copy-start = (s32[32,8]{0,1:T(8,128)S(1)}, s32[32,8]{0,1:T(8,128)}, u32[]{:S(2)}) copy-start(s32[32,8]{0,1:T(8,128)} %param.19) | copy-start | bytes 3076
  35.2 20.7 %all-to-all-start.8 = ((bf16[1,32,4,1,256]{4,2,3,0,1:T(4,128)(2,1)}), bf16[1,32,4,1,256]{4,2,3,0,1:T(4,128)(2,1)S(1)}, u32[]{:S(2)}, u32[]{:S(2)}) async-start(bf16[1,32,4,1,256]{4,2,3,0,1:T(4,128)(2,1)} %bitcast.57), calls=%async_computation.8 | async-start | bytes 131072 | tf_op jit(solution)/shard_map/all_to_all | solution.py:65
  55.8 13.1 %all-to-all-start.2 = ((bf16[1,32,4,1,256]{4,2,3,0,1:T(4,128)(2,1)}), bf16[1,32,4,1,256]{4,2,3,0,1:T(4,128)(2,1)S(1)}, u32[]{:S(2)}, u32[]{:S(2)}) async-start(bf16[1,32,4,1,256]{4,2,3,0,1:T(4,128)(2,1)} %bitcast.18), calls=%async_computation.2 | async-start | bytes 131072 | tf_op jit(solution)/shard_map/all_to_all | solution.py:65
  68.9 14.9 %all-to-all-start.11 = ((bf16[1,32,4,1,256]{4,2,3,0,1:T(4,128)(2,1)}), bf16[1,32,4,1,256]{4,2,3,0,1:T(4,128)(2,1)}, u32[]{:S(2)}, u32[]{:S(2)}) async-start(bf16[1,32,4,1,256]{4,2,3,0,1:T(4,128)(2,1)} %bitcast.74), calls=%async_computation.11 | async-start | bytes 131072 | tf_op jit(solution)/shard_map/all_to_all | solution.py:65
  80.6 22.6 %copy-start.13 = (pred[384]{0:T(512)(128)(4,1)S(1)}, pred[384]{0:T(512)(128)(4,1)}, u32[]{:S(2)}) copy-start(pred[384]{0:T(512)(128)(4,1)} %get-tuple-element.38) | copy-start | bytes 1156
  83.8 13.2 %all-to-all-start.5 = ((bf16[1,32,4,1,256]{4,2,3,0,1:T(4,128)(2,1)}), bf16[1,32,4,1,256]{4,2,3,0,1:T(4,128)(2,1)S(1)}, u32[]{:S(2)}, u32[]{:S(2)}) async-start(bf16[1,32,4,1,256]{4,2,3,0,1:T(4,128)(2,1)} %bitcast.40), calls=%async_computation.5 | async-start | bytes 131072 | tf_op jit(solution)/shard_map/all_to_all | solution.py:65
  91.3 24.0 %copy-start.12 = (pred[1792]{0:T(1024)(128)(4,1)S(1)}, pred[1792]{0:T(1024)(128)(4,1)}, u32[]{:S(2)}) copy-start(pred[1792]{0:T(1024)(128)(4,1)} %get-tuple-element.16) | copy-start | bytes 5380
  97.6 12.2 %all-to-all-start = ((bf16[1,32,4,1,768]{4,2,3,0,1:T(4,128)(2,1)}), bf16[1,32,4,1,768]{4,2,3,0,1:T(4,128)(2,1)S(1)}, u32[]{:S(2)}, u32[]{:S(2)}) async-start(bf16[1,32,4,1,768]{4,2,3,0,1:T(4,128)(2,1)} %bitcast.6), calls=%async_computation | async-start | bytes 393216 | tf_op jit(solution)/shard_map/all_to_all | solution.py:65
  109.8 5.5 %copy-start.1 = (bf16[1,32,4,1,768]{4,2,3,0,1:T(4,128)(2,1)}, bf16[1,32,4,1,768]{4,2,3,0,1:T(4,128)(2,1)S(1)}, u32[]{:S(2)}) copy-start(bf16[1,32,4,1,768]{4,2,3,0,1:T(4,128)(2,1)S(1)} %all-to-all-done) | copy-start | bytes 589828
  109.8 12.1 %all-to-all-start.3 = ((bf16[1,32,4,1,768]{4,2,3,0,1:T(4,128)(2,1)}), bf16[1,32,4,1,768]{4,2,3,0,1:T(4,128)(2,1)S(1)}, u32[]{:S(2)}, u32[]{:S(2)}) async-start(bf16[1,32,4,1,768]{4,2,3,0,1:T(4,128)(2,1)} %bitcast.28), calls=%async_computation.3 | async-start | bytes 393216 | tf_op jit(solution)/shard_map/all_to_all | solution.py:65
  115.6 11.7 %copy-start.10 = (s32[1,1792,1]{1,2,0:T(1,128)S(1)}, s32[1,1792,1]{1,2,0:T(1,128)}, u32[]{:S(2)}) copy-start(s32[1,1792,1]{1,2,0:T(1,128)} %get-tuple-element.35) | copy-start | bytes 21508
  121.9 11.0 %copy-start.4 = (bf16[1,32,4,1,768]{4,2,3,0,1:T(4,128)(2,1)}, bf16[1,32,4,1,768]{4,2,3,0,1:T(4,128)(2,1)S(1)}, u32[]{:S(2)}) copy-start(bf16[1,32,4,1,768]{4,2,3,0,1:T(4,128)(2,1)S(1)} %all-to-all-done.3) | copy-start | bytes 589828
  121.9 18.8 %all-to-all-start.6 = ((bf16[1,32,4,1,3584]{4,2,3,0,1:T(4,128)(2,1)}), bf16[1,32,4,1,3584]{4,2,3,0,1:T(4,128)(2,1)S(1)}, u32[]{:S(2)}, u32[]{:S(2)}) async-start(bf16[1,32,4,1,3584]{4,2,3,0,1:T(4,128)(2,1)} %bitcast.45), calls=%async_computation.6 | async-start | bytes 1835008 | tf_op jit(solution)/shard_map/all_to_all | solution.py:65
  127.4 5.5 %copy-start.11 = (pred[1792]{0:T(1024)(128)(4,1)S(1)}, pred[1792]{0:T(1024)(128)(4,1)}, u32[]{:S(2)}) copy-start(pred[1792]{0:T(1024)(128)(4,1)} %get-tuple-element.34) | copy-start | bytes 5380
  133.2 14.1 %copy-start.2 = (bf16[1,32,4,1,768]{4,2,3,0,1:T(4,128)(2,1)S(1)}, bf16[1,32,4,1,768]{4,2,3,0,1:T(4,128)(2,1)}, u32[]{:S(2)}) copy-start(bf16[1,32,4,1,768]{4,2,3,0,1:T(4,128)(2,1)} %copy-done.1) | copy-start | bytes 589828
  134.5 12.9 %copy-start.5 = (bf16[1,32,4,1,768]{4,2,3,0,1:T(4,128)(2,1)S(1)}, bf16[1,32,4,1,768]{4,2,3,0,1:T(4,128)(2,1)}, u32[]{:S(2)}) copy-start(bf16[1,32,4,1,768]{4,2,3,0,1:T(4,128)(2,1)} %copy-done.4) | copy-start | bytes 589828
  140.7 19.8 %all-to-all-start.9 = ((bf16[1,32,4,1,3584]{4,2,3,0,1:T(4,128)(2,1)}), bf16[1,32,4,1,3584]{4,2,3,0,1:T(4,128)(2,1)S(1)}, u32[]{:S(2)}, u32[]{:S(2)}) async-start(bf16[1,32,4,1,3584]{4,2,3,0,1:T(4,128)(2,1)} %bitcast.62), calls=%async_computation.9 | async-start | bytes 1835008 | tf_op jit(solution)/shard_map/all_to_all | solution.py:65
  160.5 19.0 %all-to-all-start.1 = ((bf16[1,4,8,4,1,768]{5,3,1,4,0,2:T(4,128)(2,1)}), bf16[1,4,8,4,1,768]{5,3,1,4,0,2:T(4,128)(2,1)S(1)}, u32[]{:S(2)}, u32[]{:S(2)}) async-start(bf16[1,4,8,4,1,768]{5,3,1,4,0,2:T(4,128)(2,1)} %get-tuple-element.46), calls=%async_computation.1 | async-start | bytes 393216 | tf_op jit(solution)/shard_map/all_to_all | solution.py:85
  179.4 6.6 %copy-start.3 = (bf16[1,4,8,4,1,768]{5,3,1,4,0,2:T(4,128)(2,1)}, bf16[1,4,8,4,1,768]{5,3,1,4,0,2:T(4,128)(2,1)S(1)}, u32[]{:S(2)}) copy-start(bf16[1,4,8,4,1,768]{5,3,1,4,0,2:T(4,128)(2,1)S(1)} %all-to-all-done.1) | copy-start | bytes 589828
  179.4 14.4 %all-to-all-start.4 = ((bf16[1,4,8,4,1,768]{5,3,1,4,0,2:T(4,128)(2,1)}), bf16[1,4,8,4,1,768]{5,3,1,4,0,2:T(4,128)(2,1)S(1)}, u32[]{:S(2)}, u32[]{:S(2)}) async-start(bf16[1,4,8,4,1,768]{5,3,1,4,0,2:T(4,128)(2,1)} %get-tuple-element.47), calls=%async_computation.4 | async-start | bytes 393216 | tf_op jit(solution)/shard_map/all_to_all | solution.py:85
  193.8 27.8 %copy-start.6 = (bf16[1,4,8,4,1,768]{5,3,1,4,0,2:T(4,128)(2,1)}, bf16[1,4,8,4,1,768]{5,3,1,4,0,2:T(4,128)(2,1)S(1)}, u32[]{:S(2)}) copy-start(bf16[1,4,8,4,1,768]{5,3,1,4,0,2:T(4,128)(2,1)S(1)} %all-to-all-done.4) | copy-start | bytes 589828
  221.6 141.6 %all-to-all-start.10 = ((bf16[1,4,8,4,1,3584]{5,3,1,4,0,2:T(4,128)(2,1)}), bf16[1,4,8,4,1,3584]{5,3,1,4,0,2:T(4,128)(2,1)S(1)}, u32[]{:S(2)}, u32[]{:S(2)}) async-start(bf16[1,4,8,4,1,3584]{5,3,1,4,0,2:T(4,128)(2,1)} %get-tuple-element.45), calls=%async_computation.10 | async-start | bytes 1835008 | tf_op jit(solution)/shard_map/all_to_all | solution.py:88
  268.6 26.0 %copy-start.9 = (bf16[1,32,4,1,256]{4,2,3,0,1:T(4,128)(2,1)S(1)}, bf16[1,32,4,1,256]{4,2,3,0,1:T(4,128)(2,1)}, u32[]{:S(2)}) copy-start(bf16[1,32,4,1,256]{4,2,3,0,1:T(4,128)(2,1)} %copy-done.8) | copy-start | bytes 196612
  358.5 1.3 copy-start.7
  (1 other events, 0.6 us)
where the time goes:
time: 373 us; the launch traced here: 372 us
  blocking collectives  146 us (39%)
  local copies, waits for them, and re-layouts  85.3 us (23%)
  starting transfers between devices  69.7 us (19%)
  waiting for transfers between devices  49.5 us (13%)
  other arithmetic  15.4 us (4%)
  matrix products  4.9 us (1%)
    all_gather x2, blocking collectives, refresh(): lax.all_gather(key_part, 'tp', axis=3, tiled=True)  67.1 us
    all_to_all x8, starting transfers between devices, refresh(): lax.all_to_all(for_sending(pieces), 'fsdp', split_axis=1, concat_axis=3,...  51.5 us
    all_gather x2, blocking collectives, refresh(): lax.all_gather(value_part, 'tp', axis=3, tiled=True)  50.7 us
    all_to_all x8, waiting for transfers between devices, refresh(): lax.all_to_all(for_sending(pieces), 'fsdp', split_axis=1, concat_axis=3,...  34.7 us
    slice x1, local copies, waits for them, and re-layouts, per_device(): learner_flat[layer_id:layer_id + 1]  28.8 us
    all_to_all x1, blocking collectives, refresh(): lax.all_to_all(to_send(out_part, widths[3]), 'tp', split_axis=2, concat_a...  27.8 us
    gather x8, local copies, waits for them, and re-layouts, cut_pieces(): picked = jnp.take_along_axis(row_table, row_ids[:, :, None], axis=1)  18.4 us
    all_to_all x2, waiting for transfers between devices, refresh(): lax.all_to_all(to_send(query_part, widths[0]), 'tp', split_axis=2, concat...  14.8 us
  transfers between devices with their start and end apart: 11, of which 8 were waited for; matrix products, arithmetic and copies ran while one was open for 17% of the time, Pallas kernels for 0%

commit v1 on v0

v1 whole, which is shorter than its diff:
```python
import functools

import jax
import jax.numpy as jnp
from jax import lax
from jax.experimental import pallas as pl
from jax.experimental.pallas import tpu as pltpu
from jax.sharding import PartitionSpec as P

MESH = pl.DeviceIdType.MESH

LANES = 128
D = 7168
QR = 1536
KVR = 512
QK_NOPE = 128
V_DIM = 128
LAYERS = 2
HEADS = 128
FSDP = 32
TP = 8
PER_GROUP = HEADS // FSDP
RANKS = FSDP * TP
Q_ROWS = QR * QK_NOPE // RANKS // LANES
KV_ROWS = QK_NOPE * KVR // RANKS // LANES
O_ROWS = D * V_DIM // RANKS // LANES
SHARD_ROWS = HEADS * (Q_ROWS + 2 * KV_ROWS + O_ROWS)
CHUNKS = LAYERS * PER_GROUP
QUARTER = FSDP // TP
PAD = 16


def gather_kernel(owner, offs, x_ref, chunk_ref, small_ref, flat, small, count):
    step_rows = 512

    def widen(i, carry):
        at = pl.multiple_of(i * step_rows, step_rows)
        flat[pl.ds(PAD + at, step_rows), :] = x_ref[pl.ds(at, step_rows), :].astype(jnp.float32)
        return carry

    lax.fori_loop(0, LAYERS * SHARD_ROWS // step_rows, widen, 0)

    def clear(i, carry):
        count[i] = 0
        return carry

    lax.fori_loop(0, LAYERS * FSDP, clear, 0)
    low = lax.broadcasted_iota(jnp.int32, (8, LANES), 0) < 4

    for l in range(LAYERS):

        def one_head(h, carry, l=l):
            f = owner[l, h]
            j = count[l * FSDP + f]
            count[l * FSDP + f] = j + 1
            starts = [PAD + l + 2 * (offs[l, k, h] // LANES) for k in range(4)]

            def rows(k, first, n):
                return flat[pl.ds(starts[k] + 2 * first, n, stride=2), :]

            for i in range(3):
                chunk_ref[l, j, f, i] = rows(3, 8 * i, 8).astype(jnp.bfloat16)
            mixed = jnp.where(low, rows(3, 24, 8), rows(0, -4, 8))
            chunk_ref[l, j, f, 3] = mixed.astype(jnp.bfloat16)
            base = (l * FSDP + f) * 24
            small[pl.ds(base + 2 * j, 2), :] = rows(0, 4, 2)
            small[pl.ds(base + 8 + 4 * j, 2), :] = rows(1, 0, 2)
            small[pl.ds(base + 10 + 4 * j, 2), :] = rows(2, 0, 2)
            return carry

        lax.fori_loop(0, HEADS, one_head, 0, unroll=4)

    for l in range(LAYERS):

        def narrow(f, carry, l=l):
            at = pl.multiple_of((l * FSDP + f) * 24, 8)
            small_ref[l, f] = small[pl.ds(at, 24), :].astype(jnp.bfloat16).reshape(3, 8, LANES)
            return carry

        lax.fori_loop(0, FSDP, narrow, 0)


def gather(owner_map, param_offsets, learner_flat):
    x = learner_flat.reshape(LAYERS, SHARD_ROWS, LANES).transpose(1, 0, 2).reshape(LAYERS * SHARD_ROWS, LANES)
    vmem = pl.BlockSpec(memory_space=pltpu.VMEM)
    smem = pl.BlockSpec(memory_space=pltpu.SMEM)
    return pl.pallas_call(
        gather_kernel,
        out_shape=(
            jax.ShapeDtypeStruct((LAYERS, PER_GROUP, FSDP, 4, 8, LANES), jnp.bfloat16),
            jax.ShapeDtypeStruct((LAYERS, FSDP, 3, 8, LANES), jnp.bfloat16),
        ),
        in_specs=[smem, smem, vmem],
        out_specs=(vmem, vmem),
        scratch_shapes=[
            pltpu.VMEM((LAYERS * SHARD_ROWS + 2 * PAD, LANES), jnp.float32),
            pltpu.VMEM((LAYERS * FSDP * 24, LANES), jnp.float32),
            pltpu.SMEM((LAYERS * FSDP,), jnp.int32),
        ],
        compiler_params=pltpu.CompilerParams(vmem_limit_bytes=40 << 20),
    )(owner_map, param_offsets.transpose(0, 2, 1), x)


def exchange_kernel(slices, chunk_ref, small_ref, q_ref, o_ref, k_ref, v_ref, *scratch):
    scratch = list(scratch)

    def take(n):
        out = scratch[:n]
        del scratch[:n]
        return out

    land_chunk = take(CHUNKS)
    land_small = take(LAYERS)
    send_rows = take(CHUNKS)
    send_rest = take(LAYERS)
    got_rows = take(CHUNKS)
    got_rest = take(LAYERS)
    got_kv = take(LAYERS)
    o_wide, q_wide, kv_wide, kv_out = take(4)
    sems = take(len(scratch))
    (
        chunk_sent, chunk_here, small_sent, small_here, rows_sent, rows_here, rest_sent, rest_here, ring_sent, ring_here, own_here,
    ) = sems

    f = lax.axis_index("fsdp")
    t = lax.axis_index("tp")

    barrier = pltpu.get_barrier_semaphore()

    def greet_plane(d, carry):
        pl.semaphore_signal(barrier, inc=1, device_id=(lax.rem(f + d, FSDP), t), device_id_type=MESH)
        return carry

    def greet_line(d, carry):
        pl.semaphore_signal(barrier, inc=1, device_id=(f, lax.rem(t + d, TP)), device_id_type=MESH)
        return carry

    lax.fori_loop(1, FSDP, greet_plane, 0)
    lax.fori_loop(1, TP, greet_line, 0)
    pl.semaphore_wait(barrier, FSDP - 1 + TP - 1)

    def remote(src, dst, send_sem, recv_sem, device):
        return pltpu.make_async_remote_copy(
            src_ref=src, dst_ref=dst, send_sem=send_sem, recv_sem=recv_sem, device_id=device, device_id_type=MESH
        )

    def spread_plane(src, dst, send_sem, recv_sem):
        pltpu.make_async_copy(src.at[f], dst.at[f], recv_sem).start()

        def one(d, carry):
            to = lax.rem(f + d, FSDP)
            remote(src.at[to], dst.at[f], send_sem, recv_sem, (to, t)).start()
            return carry

        lax.fori_loop(1, FSDP, one, 0)

    def spread_line(src, dst, send_sem, recv_sem):
        pltpu.make_async_copy(src.at[t], dst.at[t], recv_sem).start()

        def one(d, carry):
            to = lax.rem(t + d, TP)
            remote(src.at[to], dst.at[t], send_sem, recv_sem, (f, to)).start()
            return carry

        lax.fori_loop(1, TP, one, 0)

    def all_arrived(dst, recv_sem):
        pltpu.make_async_copy(dst, dst, recv_sem).wait()

    def all_left(src, n, send_sem):
        pltpu.make_async_copy(src.at[pl.ds(0, n)], src.at[pl.ds(0, n)], send_sem).wait()

    def send_small(l):
        spread_plane(small_ref.at[l], land_small[l], small_sent.at[l], small_here.at[l])

    def send_chunk(c):
        spread_plane(chunk_ref.at[c // PER_GROUP, c % PER_GROUP], land_chunk[c], chunk_sent.at[c], chunk_here.at[c])

    def forward_rows(c):
        all_arrived(land_chunk[c], chunk_here.at[c])

        def one(to, carry):
            first = slices[f, to] * QUARTER
            for q in range(QUARTER):
                send_rows[c][to, pl.ds(4 * q, 4)] = land_chunk[c][first + q]
            return carry

        lax.fori_loop(0, TP, one, 0)
        spread_line(send_rows[c], got_rows[c], rows_sent.at[c], rows_here.at[c])

    def forward_rest(l):
        def one(to, carry):
            first = slices[f, to] * QUARTER
            for q in range(QUARTER):
                send_rest[l][to, q] = land_small[l][first + q, 0]
            return carry

        lax.fori_loop(0, TP, one, 0)
        spread_line(send_rest[l], got_rest[l], rest_sent.at[l], rest_here.at[l])

    half = FSDP // 2
    steps = TP // 2
    up = lax.rem(t + 1, TP)
    down = lax.rem(t + TP - 1, TP)

    def ring_copy(l, direction, step):
        origin = lax.rem(t + (TP - step if direction == 0 else step), TP)
        if step == steps - 1:
            part = pl.ds(0, half) if direction == 0 else pl.ds(half, half)
        else:
            part = pl.ds(0, FSDP)
        to = got_kv[l].at[origin, part]
        src = land_small[l].at[part, pl.ds(1, 2)] if step == 0 else to
        return remote(src, to, ring_sent.at[l, direction, step], ring_here.at[l, direction, step], (f, up if direction == 0 else down))

    def ring_start(l, step):
        if step == 0:
            pltpu.make_async_copy(land_small[l].at[:, pl.ds(1, 2)], got_kv[l].at[t], own_here.at[l]).start()
        for direction in range(2):
            if step:
                ring_copy(l, direction, step - 1).wait_recv()
            ring_copy(l, direction, step).start()

    def ring_end(l):
        for direction in range(2):
            ring_copy(l, direction, steps - 1).wait_recv()
        pltpu.make_async_copy(land_small[l].at[:, pl.ds(1, 2)], got_kv[l].at[t], own_here.at[l]).wait()

    def assemble_kv(l):
        def widen(i, carry):
            ti = i // FSDP
            fi = i % FSDP
            rows = pl.ds(pl.multiple_of(i * 16, 16), 16)
            kv_wide[rows, :] = got_kv[l][ti, fi].astype(jnp.float32).reshape(16, LANES)
            return carry

        lax.fori_loop(0, TP * FSDP, widen, 0)

        def one_head(j, carry):
            for which, out_ref in ((0, k_ref), (1, v_ref)):
                for b in range(4):
                    for u in range(4):
                        first = (2 * u + b // 2) * FSDP * 16 + 4 * j + 2 * which + b % 2
                        kv_out[pl.ds(u, FSDP, stride=4), :] = kv_wide[pl.ds(first, FSDP, stride=16), :]
                    out_ref[l, j, :, pl.ds(b * LANES, LANES)] = kv_out[...].astype(jnp.bfloat16)
            return carry

        lax.fori_loop(0, PER_GROUP, one_head, 0)

    def assemble_rows(c):
        l, j = c // PER_GROUP, c % PER_GROUP
        all_arrived(got_rows[c], rows_here.at[c])
        if j == 0:
            all_arrived(got_rest[l], rest_here.at[l])

        def one(ti, carry):
            for q in range(QUARTER):
                block = got_rows[c][ti, pl.ds(4 * q, 4)].astype(jnp.float32).reshape(32, LANES)
                o_wide[pl.ds(q * TP * O_ROWS + ti * O_ROWS, O_ROWS), :] = block[:O_ROWS]
                q_wide[pl.ds(q * TP * Q_ROWS + ti * Q_ROWS, 4), :] = block[O_ROWS:]
                rest = got_rest[l][ti, q].astype(jnp.float32)
                q_wide[pl.ds(q * TP * Q_ROWS + ti * Q_ROWS + 4, 2), :] = rest[2 * j : 2 * j + 2]
            return carry

        lax.fori_loop(0, TP, one, 0)
        o_ref[l, j] = o_wide[...].astype(jnp.bfloat16)
        q_ref[l, j] = q_wide[...].astype(jnp.bfloat16)

    ahead = 2
    send_small(0)
    send_chunk(0)
    send_small(1)
    for c in range(1, ahead):
        send_chunk(c)
    for c in range(CHUNKS):
        if c + ahead < CHUNKS:
            send_chunk(c + ahead)
        if c == 0:
            all_arrived(land_small[0], small_here.at[0])
            forward_rest(0)
            ring_start(0, 0)
        forward_rows(c)
        if c == 0:
            all_arrived(land_small[1], small_here.at[1])
            forward_rest(1)
            ring_start(1, 0)
        elif c < steps:
            ring_start(0, c)
            ring_start(1, c)
        if c == steps:
            ring_end(0)
            assemble_kv(0)
        if c == steps + 1:
            ring_end(1)
            assemble_kv(1)
        if c >= 1:
            assemble_rows(c - 1)
    assemble_rows(CHUNKS - 1)

    for c in range(CHUNKS):
        all_left(land_chunk[c], FSDP - 1, chunk_sent.at[c])
        all_left(send_rows[c], TP - 1, rows_sent.at[c])
    for l in range(LAYERS):
        all_left(land_small[l], FSDP - 1, small_sent.at[l])
        all_left(send_rest[l], TP - 1, rest_sent.at[l])
        for direction in range(2):
            for step in range(steps):
                ring_copy(l, direction, step).wait_send()


def exchange(slice_map, chunks, small):
    vmem = pl.BlockSpec(memory_space=pltpu.VMEM)
    bf16 = jnp.bfloat16
    dma = pltpu.SemaphoreType.DMA
    rows_o = D // TP
    rows_q = QR // TP
    ring = (LAYERS, 2, TP // 2)
    return pl.pallas_call(
        exchange_kernel,
        out_shape=(
            jax.ShapeDtypeStruct((LAYERS, PER_GROUP, rows_q, LANES), bf16),
            jax.ShapeDtypeStruct((LAYERS, PER_GROUP, rows_o, LANES), bf16),
            jax.ShapeDtypeStruct((LAYERS, PER_GROUP, QK_NOPE, KVR), bf16),
            jax.ShapeDtypeStruct((LAYERS, PER_GROUP, V_DIM, KVR), bf16),
        ),
        in_specs=[pl.BlockSpec(memory_space=pltpu.SMEM), vmem, vmem],
        out_specs=(vmem,) * 4,
        scratch_shapes=[pltpu.VMEM((FSDP, 4, 8, LANES), bf16)] * CHUNKS
        + [pltpu.VMEM((FSDP, 3, 8, LANES), bf16)] * LAYERS
        + [pltpu.VMEM((TP, 16, 8, LANES), bf16)] * CHUNKS
        + [pltpu.VMEM((TP, 4, 8, LANES), bf16)] * LAYERS
        + [pltpu.VMEM((TP, 16, 8, LANES), bf16)] * CHUNKS
        + [pltpu.VMEM((TP, 4, 8, LANES), bf16)] * LAYERS
        + [pltpu.VMEM((TP, FSDP, 2, 8, LANES), bf16)] * LAYERS
        + [
            pltpu.VMEM((rows_o, LANES), jnp.float32),
            pltpu.VMEM((rows_q, LANES), jnp.float32),
            pltpu.VMEM((TP * FSDP * 16, LANES), jnp.float32),
            pltpu.VMEM((QK_NOPE, LANES), jnp.float32),
            dma((CHUNKS,)), dma((CHUNKS,)), dma((LAYERS,)), dma((LAYERS,)),
            dma((CHUNKS,)), dma((CHUNKS,)), dma((LAYERS,)), dma((LAYERS,)),
            dma(ring), dma(ring), dma((LAYERS,)),
        ],
        compiler_params=pltpu.CompilerParams(collective_id=0, has_side_effects=True, vmem_limit_bytes=50 << 20),
    )(slice_map, chunks, small)


def per_device(learner_flat, param_offsets, owner_map, slice_map):
    chunks, small = gather(owner_map, param_offsets, learner_flat)
    query, out, key, value = exchange(slice_map, chunks, small)

    def product(a, b):
        return jnp.einsum("lhrc,lhck->lhrk", a, b, preferred_element_type=jnp.float32).astype(jnp.bfloat16)

    return product(query, key), product(out, value)


def solution(mesh):
    placed = (P(None, ("fsdp", "tp")), P(), P(), P())
    return jax.shard_map(
        per_device,
        mesh=mesh,
        in_specs=placed,
        out_specs=(P(None, "fsdp", "tp", None), P(None, "fsdp", "tp", None)),
        check_vma=False,
    )
```

time: 373 us -> 114 us (0.31)
  the two profiles are of different devices: /device:TPU:38 before, /device:TPU:1 now
where the time goes in v1:
time: 114 us; the launch traced here: 113 us
  Pallas kernels  100 us (88%)
  matrix products  8.3 us (7%)
  local copies, waits for them, and re-layouts  4.45 us (4%)
    pallas_call x1, Pallas kernels, exchange(): pl.pallas_call(exchange_kernel, out_shape=(jax.ShapeDtypeStruct((LAYERS,...  90.4 us
    pallas_call x1, Pallas kernels, gather(): pl.pallas_call(gather_kernel, out_shape=(jax.ShapeDtypeStruct((LAYERS, PE...  9.56 us
    dot_general x2, matrix products, product(): jnp.einsum('lhrc,lhck->lhrk', a, b, preferred_element_type=jnp.float32)  8.3 us
    unnamed x11, local copies, waits for them, and re-layouts  4.45 us

profile of v1, /device:TPU:1, one launch (start us, length us, event | category | flops | bytes accessed | tf_op | source)
XLA Modules:
  0.0 113.4 jit_solution(17159238552661816312)
XLA Ops:
  0.6 0.0 copy-start
  0.6 1.7 %copy-done = bf16[2,622592]{1,0:T(2,128)(2,1)S(1)} copy-done((bf16[2,622592]{1,0:T(2,128)(2,1)S(1)}, bf16[2,622592]{1,0:T(2,128)(2,1)}, u32[]{:S(2)}) %copy-start) | copy-done | bytes 2490392
  2.3 0.0 copy-start.2
  2.3 0.7 copy-done.2
  3.0 0.0 copy-start.3
  3.0 0.7 copy-done.3
  3.7 0.0 copy-start.4
  3.7 9.6 %shard_map.59 = (bf16[2,4,32,4,8,128]{5,4,3,2,1,0:T(8,128)(2,1)S(1)}, bf16[2,32,3,8,128]{4,3,2,1,0:T(8,128)(2,1)S(1)}) custom-call(s32[2,128]{1,0:T(2,128)S(1)} %copy-done.3, s32[2,4,128]{2,1,0:T(4,128)S(1)} %bitcast.11, bf16[9728,128]{1,0:T(8,128)(2,1)S(1)} %bitcast.10), custom_call_target="tpu_custom_call" | custom-call | tf_op jit(solution)/shard_map/pallas_call | solution.py:87
  13.3 0.0 copy-start.1
  13.3 1.3 %copy-done.1 = bf16[2,4,32,4,8,128]{5,4,3,2,1,0:T(8,128)(2,1)} copy-done((bf16[2,4,32,4,8,128]{5,4,3,2,1,0:T(8,128)(2,1)}, bf16[2,4,32,4,8,128]{5,4,3,2,1,0:T(8,128)(2,1)S(1)}, u32[]{:S(2)}) %copy-start.1) | copy-done | bytes 2097176
  14.6 0.0 copy-done.4
  14.6 0.1 copy.7.slices
  14.7 90.4 %shard_map.60 = (bf16[2,4,192,128]{3,2,1,0:T(8,128)(2,1)S(1)}, bf16[2,4,896,128]{3,2,1,0:T(8,128)(2,1)}, bf16[2,4,128,512]{3,2,1,0:T(8,128)(2,1)S(1)}, bf16[2,4,128,512]{3,2,1,0:T(8,128)(2,1)S(1)}) custom-call(s32[32,8]{1,0:T(8,128)S(1)} %copy.7.slices, bf16[2,4,32,4,8,128]{5,4,3,2,1,0:T(8,128)(2,1)} %copy-done.1, ...), custom_call_target="tpu_custom_call" | custom-call | tf_op jit(solution)/shard_map/pallas_call | solution.py:318
  105.1 6.6 %convolution_convert_fusion = bf16[2,4,896,512]{3,2,1,0:T(8,128)(2,1)} fusion(bf16[2,4,896,128]{3,2,1,0:T(8,128)(2,1)} %get-tuple-element.12, bf16[2,4,128,512]{3,2,1,0:T(8,128)(2,1)S(1)} %get-tuple-element.13), kind=kOutput, calls=%fused_computation | convolution fusion | flops 943194112 | bytes 10223616 | tf_op jit(solution)/shard_map/lhrc,lhck->lhrk/dot_general | solution.py:353
  111.7 1.7 %convolution_convert_fusion.1 = bf16[2,4,192,512]{3,2,1,0:T(8,128)(2,1)} fusion(bf16[2,4,192,128]{3,2,1,0:T(8,128)(2,1)S(1)} %get-tuple-element.10, bf16[2,4,128,512]{3,2,1,0:T(8,128)(2,1)S(1)} %get-tuple-element.11), kind=kOutput, calls=%fused_computation.1 | convolution fusion | flops 202113024 | bytes 3014656 | tf_op jit(solution)/shard_map/lhrc,lhck->lhrk/dot_general | solution.py:353
Async XLA Ops:
  0.6 1.7 %copy-start = (bf16[2,622592]{1,0:T(2,128)(2,1)S(1)}, bf16[2,622592]{1,0:T(2,128)(2,1)}, u32[]{:S(2)}) copy-start(bf16[2,622592]{1,0:T(2,128)(2,1)} %param.4) | copy-start | bytes 7471108
  2.3 0.7 copy-start.2
  3.0 0.7 copy-start.3
  3.7 10.9 %copy-start.4 = (s32[32,8]{0,1:T(8,128)S(1)}, s32[32,8]{0,1:T(8,128)}, u32[]{:S(2)}) copy-start(s32[32,8]{0,1:T(8,128)} %param.7) | copy-start | bytes 3076
  13.3 1.3 %copy-start.1 = (bf16[2,4,32,4,8,128]{5,4,3,2,1,0:T(8,128)(2,1)}, bf16[2,4,32,4,8,128]{5,4,3,2,1,0:T(8,128)(2,1)S(1)}, u32[]{:S(2)}) copy-start(bf16[2,4,32,4,8,128]{5,4,3,2,1,0:T(8,128)(2,1)S(1)} %get-tuple-element.8.chunk_ref) | copy-start | bytes 6291460

commit v2 on v1

v2 whole, which is shorter than its diff:
```python
import jax
import jax.numpy as jnp
from jax import lax
from jax.experimental import pallas as pl
from jax.experimental.pallas import tpu as pltpu
from jax.sharding import PartitionSpec as P

MESH = pl.DeviceIdType.MESH
BF16 = jnp.bfloat16
F32 = jnp.float32

LANES = 128
D = 7168
QR = 1536
KVR = 512
QK_NOPE = 128
V_DIM = 128
LAYERS = 2
HEADS = 128
FSDP = 32
TP = 8
PER_GROUP = HEADS // FSDP
RANKS = FSDP * TP
Q_ROWS = QR * QK_NOPE // RANKS // LANES
KV_ROWS = QK_NOPE * KVR // RANKS // LANES
O_ROWS = D * V_DIM // RANKS // LANES
SHARD_ROWS = HEADS * (Q_ROWS + 2 * KV_ROWS + O_ROWS)
CHUNKS = LAYERS * PER_GROUP
QUARTER = FSDP // TP
PAD = 16
LOADS = 4
ROWS_O = D // TP
ROWS_Q = QR // TP
HALF = FSDP // 2
STEPS = TP // 2
QUERY, KEY, VALUE, OUT = range(4)


def refresh_kernel(slices, owner, offs, x_hbm, q_ref, o_ref, k_ref, v_ref, *scratch):
    scratch = list(scratch)

    def take(n):
        out = scratch[:n]
        del scratch[:n]
        return out

    make_chunk = take(CHUNKS)
    land_chunk = take(CHUNKS)
    send_rows = take(CHUNKS)
    got_rows = take(CHUNKS)
    (
        make_small,
        land_small,
        make_kv,
        line_kv,
        plane_kv,
        got_kv,
        send_rest,
        got_rest,
        x_buf,
        flat,
        table,
        starts,
        o_wide,
        q_wide,
        kv_wide,
        kv_out,
    ) = take(16)
    (
        load_sem, table_sem, chunk_sent, chunk_here, rows_sent, rows_here, small_sent, small_here,
        rest_sent, rest_here, plane_sent, plane_here, ring_sent, ring_here, own_here,
    ) = take(len(scratch))

    f = lax.axis_index("fsdp")
    t = lax.axis_index("tp")

    load_rows = LAYERS * SHARD_ROWS // LOADS

    def load(i):
        part = pl.ds(i * load_rows, load_rows)
        return pltpu.make_async_copy(x_hbm.at[part], x_buf.at[part], load_sem.at[i])

    for i in range(LOADS):
        load(i).start()

    barrier = pltpu.get_barrier_semaphore()

    def greet_plane(d, carry):
        pl.semaphore_signal(barrier, inc=1, device_id=(lax.rem(f + d, FSDP), t), device_id_type=MESH)
        return carry

    def greet_line(d, carry):
        pl.semaphore_signal(barrier, inc=1, device_id=(f, lax.rem(t + d, TP)), device_id_type=MESH)
        return carry

    lax.fori_loop(1, TP, greet_line, 0)
    lax.fori_loop(1, FSDP, greet_plane, 0)

    square = (HEADS, HEADS)
    down_index = lax.broadcasted_iota(jnp.int32, square, 0)
    across_index = lax.broadcasted_iota(jnp.int32, square, 1)
    for l in range(LAYERS):

        def across(row):
            return jnp.broadcast_to(row, square)

        def down(row):
            return across(row).T

        owns = owner[pl.ds(l, 1), :]
        earlier = jnp.logical_and(across(owns) == down(owns), down_index < across_index)
        slot = owns * PER_GROUP + jnp.sum(earlier.astype(jnp.int32), axis=0, keepdims=True)
        hit = down(slot) == across_index
        for kind in range(4):
            begin = jnp.sum(jnp.where(hit, down(offs[l, pl.ds(kind, 1), :]), 0), axis=0, keepdims=True)
            table[pl.ds(4 * l + kind, 1), :] = PAD + l + 2 * (begin >> 7)
    fetch = pltpu.make_async_copy(table, starts, table_sem)
    fetch.start()

    flat[pl.ds(0, PAD), :] = jnp.zeros((PAD, LANES), F32)
    flat[pl.ds(PAD + LAYERS * SHARD_ROWS, PAD), :] = jnp.zeros((PAD, LANES), F32)
    block = 304
    for i in range(LOADS):
        load(i).wait()

        def widen(n, carry, i=i):
            at = pl.multiple_of(i * load_rows + n * block, 16)
            flat[pl.ds(PAD + at, block), :] = x_buf[pl.ds(at, block), :].astype(F32)
            return carry

        lax.fori_loop(0, load_rows // block, widen, 0)
    fetch.wait()

    place = lax.broadcasted_iota(jnp.int32, (8, LANES), 0)

    def pick(l, kind, g, first):
        return flat[pl.ds(starts[4 * l + kind, g] + 2 * first, 8, stride=2), :]

    def last_query_rows(l, to):
        tile = pick(l, QUERY, to * PER_GROUP, 4)
        for j in range(1, PER_GROUP):
            tile = jnp.where(place < 2 * j, tile, pick(l, QUERY, to * PER_GROUP + j, 4 - 2 * j))
        return tile.astype(BF16)

    def key_value_rows(l, to, pair):
        tile = None
        for j in range(2):
            g = to * PER_GROUP + 2 * pair + j
            key = pick(l, KEY, g, -4 * j)
            tile = key if tile is None else jnp.where(place < 4 * j, tile, key)
            tile = jnp.where(place < 4 * j + 2, tile, pick(l, VALUE, g, -4 * j - 2))
        return tile.astype(BF16)

    def gather_kv(to, carry):
        for pair in range(2):
            make_kv[to, pair] = key_value_rows(0, to, pair)
        return carry

    def gather_small(to, carry):
        for l in range(LAYERS):
            make_small[to, l] = last_query_rows(l, to)
        for pair in range(2):
            make_small[to, 2 + pair] = key_value_rows(1, to, pair)
        return carry

    def gather_chunk(c):
        l, j = c // PER_GROUP, c % PER_GROUP

        def one(to, carry):
            g = to * PER_GROUP + j
            for i in range(3):
                make_chunk[c][to, i] = pick(l, OUT, g, 8 * i).astype(BF16)
            make_chunk[c][to, 3] = jnp.where(place < 4, pick(l, OUT, g, 24), pick(l, QUERY, g, -4)).astype(BF16)
            return carry

        lax.fori_loop(0, FSDP, one, 0, unroll=2)

    def remote(src, dst, send_sem, recv_sem, device):
        return pltpu.make_async_remote_copy(
            src_ref=src, dst_ref=dst, send_sem=send_sem, recv_sem=recv_sem, device_id=device, device_id_type=MESH
        )

    def spread_plane(src, dst, send_sem, recv_sem):
        pltpu.make_async_copy(src.at[f], dst.at[f], recv_sem).start()

        def one(d, carry):
            to = lax.rem(f + d, FSDP)
            remote(src.at[to], dst.at[f], send_sem, recv_sem, (to, t)).start()
            return carry

        lax.fori_loop(1, FSDP, one, 0)

    def spread_line(src, dst, send_sem, recv_sem):
        for d in (4, 1, 7, 2, 6, 3, 5):
            to = lax.rem(t + d, TP)
            remote(src.at[to], dst.at[t], send_sem, recv_sem, (f, to)).start()
        pltpu.make_async_copy(src.at[t], dst.at[t], recv_sem).start()

    def all_arrived(dst, recv_sem):
        pltpu.make_async_copy(dst, dst, recv_sem).wait()

    def all_left(src, n, send_sem):
        pltpu.make_async_copy(src.at[pl.ds(0, n)], src.at[pl.ds(0, n)], send_sem).wait()

    def send_chunk(c):
        spread_plane(make_chunk[c], land_chunk[c], chunk_sent.at[c], chunk_here.at[c])

    def forward_rows(c):
        all_arrived(land_chunk[c], chunk_here.at[c])

        def one(to, carry):
            first = slices[to, f] * QUARTER
            for q in range(QUARTER):
                send_rows[c][to, pl.ds(4 * q, 4)] = land_chunk[c][first + q]
            return carry

        lax.fori_loop(0, TP, one, 0)
        spread_line(send_rows[c], got_rows[c], rows_sent.at[c], rows_here.at[c])

    def forward_rest():
        def one(to, carry):
            first = slices[to, f] * QUARTER
            for q in range(QUARTER):
                send_rest[to, q] = land_small[first + q, pl.ds(0, 2)]
            return carry

        lax.fori_loop(0, TP, one, 0)
        spread_line(send_rest, got_rest, rest_sent.at[0], rest_here.at[0])

    up = lax.rem(t + 1, TP)
    down_to = lax.rem(t + TP - 1, TP)
    ring_own = (make_kv, land_small.at[:, pl.ds(2, 2)])
    ring_got = (line_kv, got_kv)

    def ring_copy(l, direction, step):
        origin = lax.rem(t + (TP - step if direction == 0 else step), TP)
        if step == STEPS - 1:
            part = pl.ds(0, HALF) if direction == 0 else pl.ds(HALF, HALF)
        else:
            part = pl.ds(0, FSDP)
        dst = ring_got[l].at[origin, part]
        src = dst
        if step == 0:
            src = make_kv.at[part] if l == 0 else land_small.at[part, pl.ds(2, 2)]
        to = up if direction == 0 else down_to
        return remote(src, dst, ring_sent.at[l, direction, step], ring_here.at[l, direction, step], (f, to))

    def ring_own_copy(l):
        return pltpu.make_async_copy(ring_own[l], ring_got[l].at[t], own_here.at[l])

    def ring_start(l, step):
        for direction in range(2):
            if step:
                ring_copy(l, direction, step - 1).wait_recv()
            ring_copy(l, direction, step).start()
        if step == 0:
            ring_own_copy(l).start()

    def ring_end(l):
        for direction in range(2):
            ring_copy(l, direction, STEPS - 1).wait_recv()
        ring_own_copy(l).wait()

    def spread_kv():
        pltpu.make_async_copy(line_kv.at[:, f], plane_kv.at[f], plane_here.at[0]).start()

        def one(d, carry):
            to = lax.rem(f + d, FSDP)
            remote(line_kv.at[:, to], plane_kv.at[f], plane_sent.at[0], plane_here.at[0], (to, t)).start()
            return carry

        lax.fori_loop(1, FSDP, one, 0)

    def assemble_kv(l):
        src = plane_kv if l == 0 else got_kv
        inner = src.shape[1]
        f_step, t_step = (TP, 1) if l == 0 else (1, FSDP)

        def widen(i, carry):
            rows = pl.ds(pl.multiple_of(i * 16, 16), 16)
            kv_wide[rows, :] = src[i // inner, i % inner].astype(F32).reshape(16, LANES)
            return carry

        lax.fori_loop(0, TP * FSDP, widen, 0, unroll=4)

        def one_head(j, carry):
            for which, out_ref in ((0, k_ref), (1, v_ref)):
                for b in range(4):
                    for u in range(4):
                        first = (2 * u + b // 2) * t_step * 16 + 4 * j + 2 * which + b % 2
                        kv_out[pl.ds(u, FSDP, stride=4), :] = kv_wide[pl.ds(first, FSDP, stride=16 * f_step), :]
                    out_ref[l, j, :, pl.ds(b * LANES, LANES)] = kv_out[...].astype(BF16)
            return carry

        lax.fori_loop(0, PER_GROUP, one_head, 0)

    def assemble_rows(c):
        l, j = c // PER_GROUP, c % PER_GROUP
        all_arrived(got_rows[c], rows_here.at[c])

        def one(ti, carry):
            for q in range(QUARTER):
                block = got_rows[c][ti, pl.ds(4 * q, 4)].astype(F32).reshape(32, LANES)
                o_wide[pl.ds(q * TP * O_ROWS + ti * O_ROWS, O_ROWS), :] = block[:O_ROWS]
                q_wide[pl.ds(q * TP * Q_ROWS + ti * Q_ROWS, 4), :] = block[O_ROWS:]
                rest = got_rest[ti, q, l].astype(F32)
                q_wide[pl.ds(q * TP * Q_ROWS + ti * Q_ROWS + 4, 2), :] = rest[2 * j : 2 * j + 2]
            return carry

        lax.fori_loop(0, TP, one, 0)
        o_ref[l, j] = o_wide[...].astype(BF16)
        q_ref[l, j] = q_wide[...].astype(BF16)

    lax.fori_loop(0, FSDP, gather_kv, 0, unroll=2)
    pl.semaphore_wait(barrier, FSDP - 1 + TP - 1)
    ring_start(0, 0)
    lax.fori_loop(0, FSDP, gather_small, 0)
    spread_plane(make_small, land_small, small_sent.at[0], small_here.at[0])
    ahead = 2
    for c in range(ahead):
        gather_chunk(c)
        send_chunk(c)
    ring_start(0, 1)
    all_arrived(land_small, small_here.at[0])
    ring_start(1, 0)
    forward_rest()
    for c in range(CHUNKS):
        if c + ahead < CHUNKS:
            gather_chunk(c + ahead)
            send_chunk(c + ahead)
        forward_rows(c)
        if c == 0:
            all_arrived(got_rest, rest_here.at[0])
            ring_start(0, 2)
        elif c == 1:
            ring_start(1, 1)
            ring_start(0, 3)
        elif c == 2:
            ring_end(0)
            spread_kv()
            ring_start(1, 2)
        elif c == 3:
            ring_start(1, 3)
        elif c == 4:
            all_arrived(plane_kv, plane_here.at[0])
            assemble_kv(0)
        elif c == 5:
            ring_end(1)
            assemble_kv(1)
        if c >= 2:
            assemble_rows(c - 2)
    assemble_rows(CHUNKS - 2)
    assemble_rows(CHUNKS - 1)

    for c in range(CHUNKS):
        all_left(land_chunk[c], FSDP - 1, chunk_sent.at[c])
        all_left(send_rows[c], TP - 1, rows_sent.at[c])
    all_left(land_small, FSDP - 1, small_sent.at[0])
    all_left(plane_kv, FSDP - 1, plane_sent.at[0])
    all_left(send_rest, TP - 1, rest_sent.at[0])
    for l in range(LAYERS):
        for direction in range(2):
            for step in range(STEPS):
                ring_copy(l, direction, step).wait_send()


def collect(learner_flat, param_offsets, owner_map, slice_map):
    x = learner_flat.reshape(LAYERS, SHARD_ROWS, LANES).transpose(1, 0, 2).reshape(LAYERS * SHARD_ROWS, LANES)
    vmem = pl.BlockSpec(memory_space=pltpu.VMEM)
    dma = pltpu.SemaphoreType.DMA
    ring = (LAYERS, 2, STEPS)
    chunk = pltpu.VMEM((FSDP, 4, 8, LANES), BF16)
    rows = pltpu.VMEM((TP, 4 * QUARTER, 8, LANES), BF16)
    rest = pltpu.VMEM((TP, QUARTER, 2, 8, LANES), BF16)
    by_line = pltpu.VMEM((TP, FSDP, 2, 8, LANES), BF16)
    return pl.pallas_call(
        refresh_kernel,
        out_shape=(
            jax.ShapeDtypeStruct((LAYERS, PER_GROUP, ROWS_Q, LANES), BF16),
            jax.ShapeDtypeStruct((LAYERS, PER_GROUP, ROWS_O, LANES), BF16),
            jax.ShapeDtypeStruct((LAYERS, PER_GROUP, QK_NOPE, KVR), BF16),
            jax.ShapeDtypeStruct((LAYERS, PER_GROUP, V_DIM, KVR), BF16),
        ),
        in_specs=[pl.BlockSpec(memory_space=pltpu.SMEM), vmem, vmem, pl.BlockSpec(memory_space=pltpu.HBM)],
        out_specs=(vmem,) * 4,
        scratch_shapes=[chunk] * (2 * CHUNKS)
        + [rows] * (2 * CHUNKS)
        + [
            chunk,
            chunk,
            pltpu.VMEM((FSDP, 2, 8, LANES), BF16),
            by_line,
            pltpu.VMEM((FSDP, TP, 2, 8, LANES), BF16),
            by_line,
            rest,
            rest,
            pltpu.VMEM((LAYERS * SHARD_ROWS, LANES), BF16),
            pltpu.VMEM((LAYERS * SHARD_ROWS + 2 * PAD, LANES), F32),
            pltpu.VMEM((LAYERS * 4, HEADS), jnp.int32),
            pltpu.SMEM((LAYERS * 4, HEADS), jnp.int32),
            pltpu.VMEM((ROWS_O, LANES), F32),
            pltpu.VMEM((ROWS_Q, LANES), F32),
            pltpu.VMEM((TP * FSDP * 16, LANES), F32),
            pltpu.VMEM((QK_NOPE, LANES), F32),
            dma((LOADS,)), dma, dma((CHUNKS,)), dma((CHUNKS,)), dma((CHUNKS,)), dma((CHUNKS,)), dma((1,)), dma((1,)),
            dma((1,)), dma((1,)), dma((1,)), dma((1,)), dma(ring), dma(ring), dma((LAYERS,)),
        ],
        compiler_params=pltpu.CompilerParams(collective_id=0, has_side_effects=True, vmem_limit_bytes=32 << 20),
    )(*(pltpu.with_memory_space_constraint(a, pltpu.HBM) for a in (slice_map.T, owner_map, param_offsets.transpose(0, 2, 1), x)))


def product_kernel(q_ref, o_ref, k_ref, v_ref, q_out, o_out, q_buf, o_buf, q_sem, o_sem):
    def leave(i):
        l, j, at = i // PER_GROUP, i % PER_GROUP, i % 2
        return (
            pltpu.make_async_copy(o_buf.at[at], o_out.at[l, j], o_sem.at[at]),
            pltpu.make_async_copy(q_buf.at[at], q_out.at[l, j], q_sem.at[at]),
        )

    for i in range(CHUNKS):
        l, j, at = i // PER_GROUP, i % PER_GROUP, i % 2
        o_copy, q_copy = leave(i)
        if i >= 2:
            for copy in leave(i - 2):
                copy.wait()
        o_buf[at] = jnp.dot(o_ref[l, j], v_ref[l, j], preferred_element_type=F32).astype(BF16)
        o_copy.start()
        q_buf[at] = jnp.dot(q_ref[l, j], k_ref[l, j], preferred_element_type=F32).astype(BF16)
        q_copy.start()
    for i in range(CHUNKS - 2, CHUNKS):
        for copy in leave(i):
            copy.wait()


def products(query, out, key, value):
    vmem = pl.BlockSpec(memory_space=pltpu.VMEM)
    hbm = pl.BlockSpec(memory_space=pltpu.HBM)
    return pl.pallas_call(
        product_kernel,
        out_shape=(
            jax.ShapeDtypeStruct((LAYERS, PER_GROUP, ROWS_Q, KVR), BF16),
            jax.ShapeDtypeStruct((LAYERS, PER_GROUP, ROWS_O, KVR), BF16),
        ),
        in_specs=[vmem] * 4,
        out_specs=(hbm, hbm),
        scratch_shapes=[
            pltpu.VMEM((2, ROWS_Q, KVR), BF16),
            pltpu.VMEM((2, ROWS_O, KVR), BF16),
            pltpu.SemaphoreType.DMA((2,)),
            pltpu.SemaphoreType.DMA((2,)),
        ],
        compiler_params=pltpu.CompilerParams(vmem_limit_bytes=4 << 20),
    )(query, out, key, value)


def per_device(learner_flat, param_offsets, owner_map, slice_map):
    return products(*collect(learner_flat, param_offsets, owner_map, slice_map))


def solution(mesh):
    placed = (P(None, ("fsdp", "tp")), P(), P(), P())
    return jax.shard_map(
        per_device,
        mesh=mesh,
        in_specs=placed,
        out_specs=(P(None, "fsdp", "tp", None), P(None, "fsdp", "tp", None)),
        check_vma=False,
    )
```

time: 114 us -> 95.1 us (0.83)
  matrix products: 8.3 us -> 0 us
  Pallas kernels: 100 us -> 94.3 us
  local copies, waits for them, and re-layouts: 4.45 us -> 0 us
    dot_general x2 -> x0, matrix products: 8.3 us -> none  [product(): jnp.einsum('lhrc,lhck->lhrk', a, b, preferred_element_type=jnp.float32)]
    pallas_call x2, Pallas kernels: 100 us -> 94.3 us  [the longest x1 88.4 us: collect(): pl.pallas_call(refresh_kernel, out_shape=(jax.ShapeDtypeStruct((LAYERS, P...]
    unnamed x11 -> x0, local copies, waits for them, and re-layouts: 4.45 us -> none
where the time goes in v2:
time: 95.1 us; the launch traced here: 95 us
  Pallas kernels  94.3 us (99%)
    pallas_call x1, Pallas kernels, collect(): pl.pallas_call(refresh_kernel, out_shape=(jax.ShapeDtypeStruct((LAYERS, P...  88.4 us
    pallas_call x1, Pallas kernels, products(): pl.pallas_call(product_kernel, out_shape=(jax.ShapeDtypeStruct((LAYERS, P...  5.88 us

profile of v2, /device:TPU:1, one launch (start us, length us, event | category | flops | bytes accessed | tf_op | source)
XLA Modules:
  0.0 95.0 jit_solution(3885436348079181406)
XLA Ops:
  0.6 88.4 %shard_map.59 = (bf16[2,4,192,128]{3,2,1,0:T(8,128)(2,1)S(1)}, bf16[2,4,896,128]{3,2,1,0:T(8,128)(2,1)S(1)}, bf16[2,4,128,512]{3,2,1,0:T(8,128)(2,1)S(1)}, bf16[2,4,128,512]{3,2,1,0:T(8,128)(2,1)S(1)}) custom-call(s32[8,32]{1,0:T(8,128)} %bitcast.8, s32[2,128]{1,0:T(2,128)} %owner.1, s32[2,4,128]{2,1,0:T(4,128)} %bitcast.9, bf16[9728,128]{1,0:T(8,128)(2,1)} %bitcast.7), custom_call_target="tpu_custom_call" | custom-call | tf_op jit(solution)/shard_map/pallas_call | solution.py:376
  89.1 5.9 %shard_map.60 = (bf16[2,4,192,512]{3,2,1,0:T(8,128)(2,1)}, bf16[2,4,896,512]{3,2,1,0:T(8,128)(2,1)}) custom-call(bf16[2,4,192,128]{3,2,1,0:T(8,128)(2,1)S(1)} %get-tuple-element.6.q_ref, bf16[2,4,896,128]{3,2,1,0:T(8,128)(2,1)S(1)} %get-tuple-element.7.o_ref, bf16[2,4,128,512]{3,2,1,0:T(8,128)(2,1)S(1)} %get-tuple-element.8.k_ref, ...), custom_call_target="tpu_custom_call" | custom-call | tf_op jit(solution)/shard_map/pallas_call | solution.py:438

commit v3 on v2

--- a/solution.py
+++ b/solution.py
@@ -68,7 +68,7 @@
     ) = take(16)
     (
         load_sem, table_sem, chunk_sent, chunk_here, rows_sent, rows_here, small_sent, small_here,
-        rest_sent, rest_here, plane_sent, plane_here, ring_sent, ring_here, own_here,
+        rest_sent, rest_here, plane_sent, plane_here, ring_sent, ring_here, own_here, line_sem,
     ) = take(len(scratch))
 
     f = lax.axis_index("fsdp")
@@ -89,11 +89,19 @@
         pl.semaphore_signal(barrier, inc=1, device_id=(lax.rem(f + d, FSDP), t), device_id_type=MESH)
         return carry
 
-    def greet_line(d, carry):
-        pl.semaphore_signal(barrier, inc=1, device_id=(f, lax.rem(t + d, TP)), device_id_type=MESH)
-        return carry
-
-    lax.fori_loop(1, TP, greet_line, 0)
+    up = lax.rem(t + 1, TP)
+    down_to = lax.rem(t + TP - 1, TP)
+
+    def tell_line(sem):
+        for to in (up, down_to):
+            pl.semaphore_signal(sem, inc=1, device_id=(f, to), device_id_type=MESH)
+
+    def line_round(step):
+        pl.semaphore_wait(line_sem.at[step], 2)
+        if step + 1 < STEPS - 1:
+            tell_line(line_sem.at[step + 1])
+
+    tell_line(barrier)
     lax.fori_loop(1, FSDP, greet_plane, 0)
 
     square = (HEADS, HEADS)
@@ -191,7 +199,7 @@
         lax.fori_loop(1, FSDP, one, 0)
 
     def spread_line(src, dst, send_sem, recv_sem):
-        for d in (4, 1, 7, 2, 6, 3, 5):
+        for d in (1, 7, 2, 6, 3, 5, 4):
             to = lax.rem(t + d, TP)
             remote(src.at[to], dst.at[t], send_sem, recv_sem, (f, to)).start()
         pltpu.make_async_copy(src.at[t], dst.at[t], recv_sem).start()
@@ -227,38 +235,39 @@
         lax.fori_loop(0, TP, one, 0)
         spread_line(send_rest, got_rest, rest_sent.at[0], rest_here.at[0])
 
-    up = lax.rem(t + 1, TP)
-    down_to = lax.rem(t + TP - 1, TP)
     ring_own = (make_kv, land_small.at[:, pl.ds(2, 2)])
     ring_got = (line_kv, got_kv)
 
-    def ring_copy(l, direction, step):
+    def ring_copy(l, direction, step, half):
         origin = lax.rem(t + (TP - step if direction == 0 else step), TP)
-        if step == STEPS - 1:
-            part = pl.ds(0, HALF) if direction == 0 else pl.ds(HALF, HALF)
-        else:
-            part = pl.ds(0, FSDP)
+        part = pl.ds(half * HALF, HALF)
         dst = ring_got[l].at[origin, part]
         src = dst
         if step == 0:
             src = make_kv.at[part] if l == 0 else land_small.at[part, pl.ds(2, 2)]
         to = up if direction == 0 else down_to
-        return remote(src, dst, ring_sent.at[l, direction, step], ring_here.at[l, direction, step], (f, to))
+        at = (l, direction, step, half)
+        return remote(src, dst, ring_sent.at[at], ring_here.at[at], (f, to))
+
+    def ring_moves(step):
+        return ((0, 0), (1, 1)) if step == STEPS - 1 else ((0, 0), (1, 0), (0, 1), (1, 1))
 
     def ring_own_copy(l):
         return pltpu.make_async_copy(ring_own[l], ring_got[l].at[t], own_here.at[l])
 
     def ring_start(l, step):
-        for direction in range(2):
+        for direction, half in ring_moves(step):
             if step:
-                ring_copy(l, direction, step - 1).wait_recv()
-            ring_copy(l, direction, step).start()
+                ring_copy(l, direction, step - 1, half).wait_recv()
+            ring_copy(l, direction, step, half).start()
         if step == 0:
             ring_own_copy(l).start()
 
     def ring_end(l):
-        for direction in range(2):
-            ring_copy(l, direction, STEPS - 1).wait_recv()
+        for direction, half in ((0, 1), (1, 0)):
+            ring_copy(l, direction, STEPS - 2, half).wait_recv()
+        for direction, half in ring_moves(STEPS - 1):
+            ring_copy(l, direction, STEPS - 1, half).wait_recv()
         ring_own_copy(l).wait()
 
     def spread_kv():
@@ -312,41 +321,44 @@
         q_ref[l, j] = q_wide[...].astype(BF16)
 
     lax.fori_loop(0, FSDP, gather_kv, 0, unroll=2)
-    pl.semaphore_wait(barrier, FSDP - 1 + TP - 1)
+    lax.fori_loop(0, FSDP, gather_small, 0)
+    for c in range(CHUNKS):
+        gather_chunk(c)
+    pl.semaphore_wait(barrier, FSDP - 1 + 2)
     ring_start(0, 0)
-    lax.fori_loop(0, FSDP, gather_small, 0)
+    tell_line(line_sem.at[0])
     spread_plane(make_small, land_small, small_sent.at[0], small_here.at[0])
-    ahead = 2
-    for c in range(ahead):
-        gather_chunk(c)
-        send_chunk(c)
+    send_chunk(0)
+    line_round(0)
     ring_start(0, 1)
+    send_chunk(1)
+    line_round(1)
     all_arrived(land_small, small_here.at[0])
     ring_start(1, 0)
+    line_round(2)
     forward_rest()
     for c in range(CHUNKS):
-        if c + ahead < CHUNKS:
-            gather_chunk(c + ahead)
-            send_chunk(c + ahead)
+        if c < 3:
+            send_chunk(2 * c + 2)
+            send_chunk(2 * c + 3)
         forward_rows(c)
         if c == 0:
-            all_arrived(got_rest, rest_here.at[0])
             ring_start(0, 2)
+            ring_start(1, 1)
         elif c == 1:
-            ring_start(1, 1)
             ring_start(0, 3)
+            ring_start(1, 2)
         elif c == 2:
+            ring_start(1, 3)
             ring_end(0)
             spread_kv()
-            ring_start(1, 2)
-        elif c == 3:
-            ring_start(1, 3)
-        elif c == 4:
+        elif c == CHUNKS - 1:
             all_arrived(plane_kv, plane_here.at[0])
             assemble_kv(0)
-        elif c == 5:
             ring_end(1)
             assemble_kv(1)
+        if c == 2:
+            all_arrived(got_rest, rest_here.at[0])
         if c >= 2:
             assemble_rows(c - 2)
     assemble_rows(CHUNKS - 2)
@@ -361,14 +373,16 @@
     for l in range(LAYERS):
         for direction in range(2):
             for step in range(STEPS):
-                ring_copy(l, direction, step).wait_send()
+                for half in range(2):
+                    if (direction, half) in ring_moves(step):
+                        ring_copy(l, direction, step, half).wait_send()
 
 
 def collect(learner_flat, param_offsets, owner_map, slice_map):
     x = learner_flat.reshape(LAYERS, SHARD_ROWS, LANES).transpose(1, 0, 2).reshape(LAYERS * SHARD_ROWS, LANES)
     vmem = pl.BlockSpec(memory_space=pltpu.VMEM)
     dma = pltpu.SemaphoreType.DMA
-    ring = (LAYERS, 2, STEPS)
+    ring = (LAYERS, 2, STEPS, 2)
     chunk = pltpu.VMEM((FSDP, 4, 8, LANES), BF16)
     rows = pltpu.VMEM((TP, 4 * QUARTER, 8, LANES), BF16)
     rest = pltpu.VMEM((TP, QUARTER, 2, 8, LANES), BF16)
@@ -404,6 +418,7 @@
             pltpu.VMEM((QK_NOPE, LANES), F32),
             dma((LOADS,)), dma, dma((CHUNKS,)), dma((CHUNKS,)), dma((CHUNKS,)), dma((CHUNKS,)), dma((1,)), dma((1,)),
             dma((1,)), dma((1,)), dma((1,)), dma((1,)), dma(ring), dma(ring), dma((LAYERS,)),
+            pltpu.SemaphoreType.REGULAR((STEPS - 1,)),
         ],
         compiler_params=pltpu.CompilerParams(collective_id=0, has_side_effects=True, vmem_limit_bytes=32 << 20),
     )(*(pltpu.with_memory_space_constraint(a, pltpu.HBM) for a in (slice_map.T, owner_map, param_offsets.transpose(0, 2, 1), x)))
@@ -411,23 +426,20 @@
 
 def product_kernel(q_ref, o_ref, k_ref, v_ref, q_out, o_out, q_buf, o_buf, q_sem, o_sem):
     def leave(i):
-        l, j, at = i // PER_GROUP, i % PER_GROUP, i % 2
+        l, j, at = i // PER_GROUP, i % PER_GROUP, i
         return (
             pltpu.make_async_copy(o_buf.at[at], o_out.at[l, j], o_sem.at[at]),
             pltpu.make_async_copy(q_buf.at[at], q_out.at[l, j], q_sem.at[at]),
         )
 
     for i in range(CHUNKS):
-        l, j, at = i // PER_GROUP, i % PER_GROUP, i % 2
-        o_copy, q_copy = leave(i)
-        if i >= 2:
-            for copy in leave(i - 2):
-                copy.wait()
-        o_buf[at] = jnp.dot(o_ref[l, j], v_ref[l, j], preferred_element_type=F32).astype(BF16)
-        o_copy.start()
+        l, j, at = i // PER_GROUP, i % PER_GROUP, i
         q_buf[at] = jnp.dot(q_ref[l, j], k_ref[l, j], preferred_element_type=F32).astype(BF16)
-        q_copy.start()
-    for i in range(CHUNKS - 2, CHUNKS):
+        pltpu.make_async_copy(q_buf.at[at], q_out.at[l, j], q_sem.at[at]).start()
+        for r in range(0, ROWS_O, 224):
+            o_buf[at, pl.ds(r, 224)] = jnp.dot(o_ref[l, j, pl.ds(r, 224)], v_ref[l, j], preferred_element_type=F32).astype(BF16)
+            pltpu.make_async_copy(o_buf.at[at, pl.ds(r, 224)], o_out.at[l, j, pl.ds(r, 224)], o_sem.at[at]).start()
+    for i in range(CHUNKS):
         for copy in leave(i):
             copy.wait()
 
@@ -444,12 +456,12 @@
         in_specs=[vmem] * 4,
         out_specs=(hbm, hbm),
         scratch_shapes=[
-            pltpu.VMEM((2, ROWS_Q, KVR), BF16),
-            pltpu.VMEM((2, ROWS_O, KVR), BF16),
-            pltpu.SemaphoreType.DMA((2,)),
-            pltpu.SemaphoreType.DMA((2,)),
+            pltpu.VMEM((CHUNKS, ROWS_Q, KVR), BF16),
+            pltpu.VMEM((CHUNKS, ROWS_O, KVR), BF16),
+            pltpu.SemaphoreType.DMA((CHUNKS,)),
+            pltpu.SemaphoreType.DMA((CHUNKS,)),
         ],
-        compiler_params=pltpu.CompilerParams(vmem_limit_bytes=4 << 20),
+        compiler_params=pltpu.CompilerParams(vmem_limit_bytes=12 << 20),
     )(query, out, key, value)
 
 

time: 95.1 us -> 90.1 us (0.947)
  Pallas kernels: 94.3 us -> 89.3 us
    pallas_call x1, Pallas kernels: 88.4 us -> 85.6 us  [collect(): pl.pallas_call(refresh_kernel, out_shape=(jax.ShapeDtypeStruct((LAYERS, P...]
    pallas_call x1, Pallas kernels: 5.88 us -> 3.75 us  [products(): pl.pallas_call(product_kernel, out_shape=(jax.ShapeDtypeStruct((LAYERS, P...]
where the time goes in v3:
time: 90.1 us; the launch traced here: 89.9 us
  Pallas kernels  89.3 us (99%)
    pallas_call x1, Pallas kernels, collect(): pl.pallas_call(refresh_kernel, out_shape=(jax.ShapeDtypeStruct((LAYERS, P...  85.6 us
    pallas_call x1, Pallas kernels, products(): pl.pallas_call(product_kernel, out_shape=(jax.ShapeDtypeStruct((LAYERS, P...  3.75 us

profile of v3, /device:TPU:1, one launch (start us, length us, event | category | flops | bytes accessed | tf_op | source)
XLA Modules:
  0.0 89.9 jit_solution(11757314922574895301)
XLA Ops:
  0.6 85.6 %shard_map.59 = (bf16[2,4,192,128]{3,2,1,0:T(8,128)(2,1)S(1)}, bf16[2,4,896,128]{3,2,1,0:T(8,128)(2,1)S(1)}, bf16[2,4,128,512]{3,2,1,0:T(8,128)(2,1)S(1)}, bf16[2,4,128,512]{3,2,1,0:T(8,128)(2,1)S(1)}) custom-call(s32[8,32]{1,0:T(8,128)} %bitcast.8, s32[2,128]{1,0:T(2,128)} %owner.1, s32[2,4,128]{2,1,0:T(4,128)} %bitcast.9, bf16[9728,128]{1,0:T(8,128)(2,1)} %bitcast.7), custom_call_target="tpu_custom_call" | custom-call | tf_op jit(solution)/shard_map/pallas_call | solution.py:390
  86.2 3.8 %shard_map.60 = (bf16[2,4,192,512]{3,2,1,0:T(8,128)(2,1)}, bf16[2,4,896,512]{3,2,1,0:T(8,128)(2,1)}) custom-call(bf16[2,4,192,128]{3,2,1,0:T(8,128)(2,1)S(1)} %get-tuple-element.6.q_ref, bf16[2,4,896,128]{3,2,1,0:T(8,128)(2,1)S(1)} %get-tuple-element.7.o_ref, bf16[2,4,128,512]{3,2,1,0:T(8,128)(2,1)S(1)} %get-tuple-element.8.k_ref, ...), custom_call_target="tpu_custom_call" | custom-call | tf_op jit(solution)/shard_map/pallas_call | solution.py:450

commit v4 on v3

--- a/solution.py
+++ b/solution.py
@@ -36,7 +36,7 @@
 QUERY, KEY, VALUE, OUT = range(4)
 
 
-def refresh_kernel(slices, owner, offs, x_hbm, q_ref, o_ref, k_ref, v_ref, *scratch):
+def refresh_kernel(slices_hbm, owner_hbm, offs_hbm, x_hbm, q_ref, o_ref, k_ref, v_ref, *scratch):
     scratch = list(scratch)
 
     def take(n):
@@ -48,13 +48,12 @@
     land_chunk = take(CHUNKS)
     send_rows = take(CHUNKS)
     got_rows = take(CHUNKS)
+    make_kv = take(LAYERS)
+    line_kv = take(LAYERS)
+    plane_kv = take(LAYERS)
     (
         make_small,
         land_small,
-        make_kv,
-        line_kv,
-        plane_kv,
-        got_kv,
         send_rest,
         got_rest,
         x_buf,
@@ -65,10 +64,13 @@
         q_wide,
         kv_wide,
         kv_out,
-    ) = take(16)
+        slices,
+        owner,
+        offs,
+    ) = take(15)
     (
         load_sem, table_sem, chunk_sent, chunk_here, rows_sent, rows_here, small_sent, small_here,
-        rest_sent, rest_here, plane_sent, plane_here, ring_sent, ring_here, own_here, line_sem,
+        rest_sent, rest_here, plane_sent, plane_here, ring_sent, ring_here, own_here, line_sem, map_sem,
     ) = take(len(scratch))
 
     f = lax.axis_index("fsdp")
@@ -79,9 +81,6 @@
     def load(i):
         part = pl.ds(i * load_rows, load_rows)
         return pltpu.make_async_copy(x_hbm.at[part], x_buf.at[part], load_sem.at[i])
-
-    for i in range(LOADS):
-        load(i).start()
 
     barrier = pltpu.get_barrier_semaphore()
 
@@ -103,6 +102,16 @@
 
     tell_line(barrier)
     lax.fori_loop(1, FSDP, greet_plane, 0)
+    maps = [
+        pltpu.make_async_copy(src, dst, map_sem.at[i])
+        for i, (src, dst) in enumerate(((owner_hbm, owner), (offs_hbm, offs), (slices_hbm, slices)))
+    ]
+    for copy in maps:
+        copy.start()
+    for i in range(LOADS):
+        load(i).start()
+    for copy in maps:
+        copy.wait()
 
     square = (HEADS, HEADS)
     down_index = lax.broadcasted_iota(jnp.int32, square, 0)
@@ -159,16 +168,17 @@
             tile = jnp.where(place < 4 * j + 2, tile, pick(l, VALUE, g, -4 * j - 2))
         return tile.astype(BF16)
 
-    def gather_kv(to, carry):
-        for pair in range(2):
-            make_kv[to, pair] = key_value_rows(0, to, pair)
-        return carry
+    def gather_kv(l):
+        def one(to, carry):
+            for pair in range(2):
+                make_kv[l][to, pair] = key_value_rows(l, to, pair)
+            return carry
+
+        lax.fori_loop(0, FSDP, one, 0, unroll=2)
 
     def gather_small(to, carry):
         for l in range(LAYERS):
             make_small[to, l] = last_query_rows(l, to)
-        for pair in range(2):
-            make_small[to, 2 + pair] = key_value_rows(1, to, pair)
         return carry
 
     def gather_chunk(c):
@@ -198,8 +208,8 @@
 
         lax.fori_loop(1, FSDP, one, 0)
 
-    def spread_line(src, dst, send_sem, recv_sem):
-        for d in (1, 7, 2, 6, 3, 5, 4):
+    def spread_line(src, dst, send_sem, recv_sem, order=(1, 7, 2, 6, 3, 5, 4)):
+        for d in order:
             to = lax.rem(t + d, TP)
             remote(src.at[to], dst.at[t], send_sem, recv_sem, (f, to)).start()
         pltpu.make_async_copy(src.at[t], dst.at[t], recv_sem).start()
@@ -223,28 +233,26 @@
             return carry
 
         lax.fori_loop(0, TP, one, 0)
-        spread_line(send_rows[c], got_rows[c], rows_sent.at[c], rows_here.at[c])
+        if c < CHUNKS - 1:
+            spread_line(send_rows[c], got_rows[c], rows_sent.at[c], rows_here.at[c])
+        else:
+            spread_line(send_rows[c], got_rows[c], rows_sent.at[c], rows_here.at[c], (4, 3, 5, 2, 6, 1, 7))
 
     def forward_rest():
         def one(to, carry):
             first = slices[to, f] * QUARTER
             for q in range(QUARTER):
-                send_rest[to, q] = land_small[first + q, pl.ds(0, 2)]
+                send_rest[to, q] = land_small[first + q]
             return carry
 
         lax.fori_loop(0, TP, one, 0)
         spread_line(send_rest, got_rest, rest_sent.at[0], rest_here.at[0])
-
-    ring_own = (make_kv, land_small.at[:, pl.ds(2, 2)])
-    ring_got = (line_kv, got_kv)
 
     def ring_copy(l, direction, step, half):
         origin = lax.rem(t + (TP - step if direction == 0 else step), TP)
         part = pl.ds(half * HALF, HALF)
-        dst = ring_got[l].at[origin, part]
-        src = dst
-        if step == 0:
-            src = make_kv.at[part] if l == 0 else land_small.at[part, pl.ds(2, 2)]
+        dst = line_kv[l].at[origin, part]
+        src = make_kv[l].at[part] if step == 0 else dst
         to = up if direction == 0 else down_to
         at = (l, direction, step, half)
         return remote(src, dst, ring_sent.at[at], ring_here.at[at], (f, to))
@@ -253,7 +261,7 @@
         return ((0, 0), (1, 1)) if step == STEPS - 1 else ((0, 0), (1, 0), (0, 1), (1, 1))
 
     def ring_own_copy(l):
-        return pltpu.make_async_copy(ring_own[l], ring_got[l].at[t], own_here.at[l])
+        return pltpu.make_async_copy(make_kv[l], line_kv[l].at[t], own_here.at[l])
 
     def ring_start(l, step):
         for direction, half in ring_moves(step):
@@ -270,24 +278,20 @@
             ring_copy(l, direction, STEPS - 1, half).wait_recv()
         ring_own_copy(l).wait()
 
-    def spread_kv():
-        pltpu.make_async_copy(line_kv.at[:, f], plane_kv.at[f], plane_here.at[0]).start()
+    def spread_kv(l):
+        pltpu.make_async_copy(line_kv[l].at[:, f], plane_kv[l].at[f], plane_here.at[l]).start()
 
         def one(d, carry):
             to = lax.rem(f + d, FSDP)
-            remote(line_kv.at[:, to], plane_kv.at[f], plane_sent.at[0], plane_here.at[0], (to, t)).start()
+            remote(line_kv[l].at[:, to], plane_kv[l].at[f], plane_sent.at[l], plane_here.at[l], (to, t)).start()
             return carry
 
         lax.fori_loop(1, FSDP, one, 0)
 
     def assemble_kv(l):
-        src = plane_kv if l == 0 else got_kv
-        inner = src.shape[1]
-        f_step, t_step = (TP, 1) if l == 0 else (1, FSDP)
-
         def widen(i, carry):
             rows = pl.ds(pl.multiple_of(i * 16, 16), 16)
-            kv_wide[rows, :] = src[i // inner, i % inner].astype(F32).reshape(16, LANES)
+            kv_wide[rows, :] = plane_kv[l][i // TP, i % TP].astype(F32).reshape(16, LANES)
             return carry
 
         lax.fori_loop(0, TP * FSDP, widen, 0, unroll=4)
@@ -296,8 +300,8 @@
             for which, out_ref in ((0, k_ref), (1, v_ref)):
                 for b in range(4):
                     for u in range(4):
-                        first = (2 * u + b // 2) * t_step * 16 + 4 * j + 2 * which + b % 2
-                        kv_out[pl.ds(u, FSDP, stride=4), :] = kv_wide[pl.ds(first, FSDP, stride=16 * f_step), :]
+                        first = (2 * u + b // 2) * 16 + 4 * j + 2 * which + b % 2
+                        kv_out[pl.ds(u, FSDP, stride=4), :] = kv_wide[pl.ds(first, FSDP, stride=16 * TP), :]
                     out_ref[l, j, :, pl.ds(b * LANES, LANES)] = kv_out[...].astype(BF16)
             return carry
 
@@ -320,43 +324,51 @@
         o_ref[l, j] = o_wide[...].astype(BF16)
         q_ref[l, j] = q_wide[...].astype(BF16)
 
-    lax.fori_loop(0, FSDP, gather_kv, 0, unroll=2)
-    lax.fori_loop(0, FSDP, gather_small, 0)
-    for c in range(CHUNKS):
-        gather_chunk(c)
+    gather_kv(0)
     pl.semaphore_wait(barrier, FSDP - 1 + 2)
     ring_start(0, 0)
     tell_line(line_sem.at[0])
+    gather_chunk(0)
+    send_chunk(0)
+    gather_kv(1)
+    ring_start(1, 0)
+    line_round(0)
+    lax.fori_loop(0, FSDP, gather_small, 0)
     spread_plane(make_small, land_small, small_sent.at[0], small_here.at[0])
-    send_chunk(0)
-    line_round(0)
-    ring_start(0, 1)
+    gather_chunk(1)
     send_chunk(1)
     line_round(1)
-    all_arrived(land_small, small_here.at[0])
-    ring_start(1, 0)
+    ring_start(0, 1)
+    gather_chunk(2)
+    gather_chunk(3)
     line_round(2)
-    forward_rest()
+    ring_start(1, 1)
     for c in range(CHUNKS):
         if c < 3:
             send_chunk(2 * c + 2)
             send_chunk(2 * c + 3)
         forward_rows(c)
+        if c < 2:
+            gather_chunk(2 * c + 4)
+            gather_chunk(2 * c + 5)
         if c == 0:
             ring_start(0, 2)
-            ring_start(1, 1)
+            all_arrived(land_small, small_here.at[0])
+            forward_rest()
+            ring_start(1, 2)
         elif c == 1:
             ring_start(0, 3)
-            ring_start(1, 2)
+            ring_start(1, 3)
         elif c == 2:
-            ring_start(1, 3)
             ring_end(0)
-            spread_kv()
+            spread_kv(0)
+        elif c == 3:
+            ring_end(1)
+            spread_kv(1)
         elif c == CHUNKS - 1:
-            all_arrived(plane_kv, plane_here.at[0])
-            assemble_kv(0)
-            ring_end(1)
-            assemble_kv(1)
+            for l in range(LAYERS):
+                all_arrived(plane_kv[l], plane_here.at[l])
+                assemble_kv(l)
         if c == 2:
             all_arrived(got_rest, rest_here.at[0])
         if c >= 2:
@@ -368,9 +380,9 @@
         all_left(land_chunk[c], FSDP - 1, chunk_sent.at[c])
         all_left(send_rows[c], TP - 1, rows_sent.at[c])
     all_left(land_small, FSDP - 1, small_sent.at[0])
-    all_left(plane_kv, FSDP - 1, plane_sent.at[0])
     all_left(send_rest, TP - 1, rest_sent.at[0])
     for l in range(LAYERS):
+        all_left(plane_kv[l], FSDP - 1, plane_sent.at[l])
         for direction in range(2):
             for step in range(STEPS):
                 for half in range(2):
@@ -386,7 +398,6 @@
     chunk = pltpu.VMEM((FSDP, 4, 8, LANES), BF16)
     rows = pltpu.VMEM((TP, 4 * QUARTER, 8, LANES), BF16)
     rest = pltpu.VMEM((TP, QUARTER, 2, 8, LANES), BF16)
-    by_line = pltpu.VMEM((TP, FSDP, 2, 8, LANES), BF16)
     return pl.pallas_call(
         refresh_kernel,
         out_shape=(
@@ -395,17 +406,16 @@
             jax.ShapeDtypeStruct((LAYERS, PER_GROUP, QK_NOPE, KVR), BF16),
             jax.ShapeDtypeStruct((LAYERS, PER_GROUP, V_DIM, KVR), BF16),
         ),
-        in_specs=[pl.BlockSpec(memory_space=pltpu.SMEM), vmem, vmem, pl.BlockSpec(memory_space=pltpu.HBM)],
+        in_specs=[pl.BlockSpec(memory_space=pltpu.HBM)] * 4,
         out_specs=(vmem,) * 4,
         scratch_shapes=[chunk] * (2 * CHUNKS)
         + [rows] * (2 * CHUNKS)
+        + [pltpu.VMEM((FSDP, 2, 8, LANES), BF16)] * LAYERS
+        + [pltpu.VMEM((TP, FSDP, 2, 8, LANES), BF16)] * LAYERS
+        + [pltpu.VMEM((FSDP, TP, 2, 8, LANES), BF16)] * LAYERS
         + [
-            chunk,
-            chunk,
-            pltpu.VMEM((FSDP, 2, 8, LANES), BF16),
-            by_line,
-            pltpu.VMEM((FSDP, TP, 2, 8, LANES), BF16),
-            by_line,
+            pltpu.VMEM((FSDP, LAYERS, 8, LANES), BF16),
+            pltpu.VMEM((FSDP, LAYERS, 8, LANES), BF16),
             rest,
             rest,
             pltpu.VMEM((LAYERS * SHARD_ROWS, LANES), BF16),
@@ -416,9 +426,12 @@
             pltpu.VMEM((ROWS_Q, LANES), F32),
             pltpu.VMEM((TP * FSDP * 16, LANES), F32),
             pltpu.VMEM((QK_NOPE, LANES), F32),
+            pltpu.SMEM((TP, FSDP), jnp.int32),
+            pltpu.VMEM((LAYERS, HEADS), jnp.int32),
+            pltpu.VMEM((LAYERS, 4, HEADS), jnp.int32),
             dma((LOADS,)), dma, dma((CHUNKS,)), dma((CHUNKS,)), dma((CHUNKS,)), dma((CHUNKS,)), dma((1,)), dma((1,)),
-            dma((1,)), dma((1,)), dma((1,)), dma((1,)), dma(ring), dma(ring), dma((LAYERS,)),
-            pltpu.SemaphoreType.REGULAR((STEPS - 1,)),
+            dma((1,)), dma((1,)), dma((LAYERS,)), dma((LAYERS,)), dma(ring), dma(ring), dma((LAYERS,)),
+            pltpu.SemaphoreType.REGULAR((STEPS - 1,)), dma((3,)),
         ],
         compiler_params=pltpu.CompilerParams(collective_id=0, has_side_effects=True, vmem_limit_bytes=32 << 20),
     )(*(pltpu.with_memory_space_constraint(a, pltpu.HBM) for a in (slice_map.T, owner_map, param_offsets.transpose(0, 2, 1), x)))

time: 90.1 us -> 86.3 us (0.958)
  Pallas kernels: 89.3 us -> 85.5 us
    pallas_call x1, Pallas kernels: 85.6 us -> 81.8 us  [collect(): pl.pallas_call(refresh_kernel, out_shape=(jax.ShapeDtypeStruct((LAYERS, P...]
where the time goes in v4:
time: 86.3 us; the launch traced here: 86.2 us
  Pallas kernels  85.5 us (99%)
    pallas_call x1, Pallas kernels, collect(): pl.pallas_call(refresh_kernel, out_shape=(jax.ShapeDtypeStruct((LAYERS, P...  81.8 us
    pallas_call x1, Pallas kernels, products(): pl.pallas_call(product_kernel, out_shape=(jax.ShapeDtypeStruct((LAYERS, P...  3.75 us

profile of v4, /device:TPU:1, one launch (start us, length us, event | category | flops | bytes accessed | tf_op | source)
XLA Modules:
  0.0 86.2 jit_solution(6257487126398073870)
XLA Ops:
  0.6 81.8 %shard_map.59 = (bf16[2,4,192,128]{3,2,1,0:T(8,128)(2,1)S(1)}, bf16[2,4,896,128]{3,2,1,0:T(8,128)(2,1)S(1)}, bf16[2,4,128,512]{3,2,1,0:T(8,128)(2,1)S(1)}, bf16[2,4,128,512]{3,2,1,0:T(8,128)(2,1)S(1)}) custom-call(s32[8,32]{1,0:T(8,128)} %bitcast.8, s32[2,128]{1,0:T(2,128)} %owner_hbm.1, s32[2,4,128]{2,1,0:T(4,128)} %bitcast.9, bf16[9728,128]{1,0:T(8,128)(2,1)} %bitcast.7), custom_call_target="tpu_custom_call" | custom-call | tf_op jit(solution)/shard_map/pallas_call | solution.py:401
  82.4 3.8 %shard_map.60 = (bf16[2,4,192,512]{3,2,1,0:T(8,128)(2,1)}, bf16[2,4,896,512]{3,2,1,0:T(8,128)(2,1)}) custom-call(bf16[2,4,192,128]{3,2,1,0:T(8,128)(2,1)S(1)} %get-tuple-element.6.q_ref, bf16[2,4,896,128]{3,2,1,0:T(8,128)(2,1)S(1)} %get-tuple-element.7.o_ref, bf16[2,4,128,512]{3,2,1,0:T(8,128)(2,1)S(1)} %get-tuple-element.8.k_ref, ...), custom_call_target="tpu_custom_call" | custom-call | tf_op jit(solution)/shard_map/pallas_call | solution.py:463

commit v5 on v4

--- a/solution.py
+++ b/solution.py
@@ -302,7 +302,7 @@
                     for u in range(4):
                         first = (2 * u + b // 2) * 16 + 4 * j + 2 * which + b % 2
                         kv_out[pl.ds(u, FSDP, stride=4), :] = kv_wide[pl.ds(first, FSDP, stride=16 * TP), :]
-                    out_ref[l, j, :, pl.ds(b * LANES, LANES)] = kv_out[...].astype(BF16)
+                    out_ref[l, j, :, pl.ds(b * LANES, LANES)] = kv_out[pl.ds(0, QK_NOPE), :].astype(BF16)
             return carry
 
         lax.fori_loop(0, PER_GROUP, one_head, 0)
@@ -424,8 +424,8 @@
             pltpu.SMEM((LAYERS * 4, HEADS), jnp.int32),
             pltpu.VMEM((ROWS_O, LANES), F32),
             pltpu.VMEM((ROWS_Q, LANES), F32),
-            pltpu.VMEM((TP * FSDP * 16, LANES), F32),
-            pltpu.VMEM((QK_NOPE, LANES), F32),
+            pltpu.VMEM((TP * FSDP * 16 + 16 * TP, LANES), F32),
+            pltpu.VMEM((QK_NOPE + 8, LANES), F32),
             pltpu.SMEM((TP, FSDP), jnp.int32),
             pltpu.VMEM((LAYERS, HEADS), jnp.int32),
             pltpu.VMEM((LAYERS, 4, HEADS), jnp.int32),

time: 86.3 us -> 86.3 us (level)
  no operation moved by 1% of the time
where the time goes in v5:
time: 86.3 us; the launch traced here: 86.2 us
  Pallas kernels  85.5 us (99%)
    pallas_call x1, Pallas kernels, collect(): pl.pallas_call(refresh_kernel, out_shape=(jax.ShapeDtypeStruct((LAYERS, P...  81.8 us
    pallas_call x1, Pallas kernels, products(): pl.pallas_call(product_kernel, out_shape=(jax.ShapeDtypeStruct((LAYERS, P...  3.75 us

profile of v5, /device:TPU:1, one launch (start us, length us, event | category | flops | bytes accessed | tf_op | source)
XLA Modules:
  0.0 86.2 jit_solution(6685964857390752900)
XLA Ops:
  0.6 81.8 %shard_map.59 = (bf16[2,4,192,128]{3,2,1,0:T(8,128)(2,1)S(1)}, bf16[2,4,896,128]{3,2,1,0:T(8,128)(2,1)S(1)}, bf16[2,4,128,512]{3,2,1,0:T(8,128)(2,1)S(1)}, bf16[2,4,128,512]{3,2,1,0:T(8,128)(2,1)S(1)}) custom-call(s32[8,32]{1,0:T(8,128)} %bitcast.8, s32[2,128]{1,0:T(2,128)} %owner_hbm.1, s32[2,4,128]{2,1,0:T(4,128)} %bitcast.9, bf16[9728,128]{1,0:T(8,128)(2,1)} %bitcast.7), custom_call_target="tpu_custom_call" | custom-call | tf_op jit(solution)/shard_map/pallas_call | solution.py:401
  82.4 3.8 %shard_map.60 = (bf16[2,4,192,512]{3,2,1,0:T(8,128)(2,1)}, bf16[2,4,896,512]{3,2,1,0:T(8,128)(2,1)}) custom-call(bf16[2,4,192,128]{3,2,1,0:T(8,128)(2,1)S(1)} %get-tuple-element.6.q_ref, bf16[2,4,896,128]{3,2,1,0:T(8,128)(2,1)S(1)} %get-tuple-element.7.o_ref, bf16[2,4,128,512]{3,2,1,0:T(8,128)(2,1)S(1)} %get-tuple-element.8.k_ref, ...), custom_call_target="tpu_custom_call" | custom-call | tf_op jit(solution)/shard_map/pallas_call | solution.py:463
